TPU v7x, 256 devices: a whole 4x4x8 slice. The times are simulated.
256 devices in a mesh: solver: 128 (over z, y, x), ana: 2 (over core).
Axes of the slice: x: 4, y: 4, z: 8, core: 2. Of those that a mesh axis runs over, the one named last changes fastest.
Arguments:
- state: float32 [8192, 320], P(('solver', 'ana')), may hold values from -68 to 68
- history: bfloat16 [124, 8192, 320], P(None, ('solver', 'ana')), may hold values from -68 to 68
- inv_mass: float32 [64, 64, 8192], P(None, None, ('solver', 'ana')), may hold values from -1 to 3
- vol_op: float32 [320, 320], replicated, may hold values from -0.3125 to 0.3125
- lift_ops: float32 [6, 80, 320], replicated, may hold values from -0.625 to 0.625
- neighbors: int32 [6, 8192], P(None, ('solver', 'ana')), may hold values from -1 to 8191, as said below
- owner: int32 [8192], P(('solver', 'ana')), may hold values from 0 to 1, as said below
Outputs:
- coef: float32 [8192, 320, 128], P(('solver', 'ana'))
- factor: float32 [2, 128, 128], P('ana')
Inputs may be any that keep to these rules, and one draw needn't show every extreme that they name: `neighbors`: the elements fill a grid of 2 x 8 x 512 cells along x (periodic), y (walls) and z (periodic); partition p = g * 2 + a holds the cells with y in a * 4 to (a + 1) * 4 - 1 and z in g * 4 to (g + 1) * 4 - 1 under the ids p * 32 to (p + 1) * 32 - 1 in some order; row f names the cell across face f, and -1 only across a wall. `owner`: every partition of 32 consecutive elements names every region exactly 16 times.
All inputs are finite; a program needn't handle non-finite values.
Results may differ from a plain program's by a relative error of at most 0.0003.
Values may be sent and summed in bfloat16 or wider, within the bound.
No kernel may reach another device: no remote copies, remote signals or barrier semaphores. Data moves between devices by JAX's collectives and lax.ppermute only.
A program may use at most 128 MiB of HBM per device.

v0:
```python
import jax
import jax.numpy as jnp
import numpy as np
from jax import lax
from jax.sharding import PartitionSpec as P

FIELDS = 5
SIDE = 4
NODES = 64
FC = 80
STEPS = 4
LX = 2
LY = 4
LZ = 4


time_step = 0.2
far_away = 1073741824


def with_halo(cells, sides, width, closed):
    for axis, dim in sides:
        count = lax.axis_size(axis)
        ends = count if closed else count - 1
        head = lax.slice_in_dim(cells, 0, width, axis=dim)
        tail = lax.slice_in_dim(cells, cells.shape[dim] - width, cells.shape[dim], axis=dim)
        cells = jnp.concatenate(
            [
                lax.ppermute(tail, axis, [(i, (i + 1) % count) for i in range(ends)]),
                cells,
                lax.ppermute(head, axis, [((i + 1) % count, i) for i in range(ends)]),
            ],
            axis=dim,
        )
    return cells


def face_table(side):
    grid = np.arange(side**3).reshape(side, side, side)
    planes = [
        grid[:, :, 0],
        grid[:, :, side - 1],
        grid[:, 0, :],
        grid[:, side - 1, :],
        grid[0, :, :],
        grid[side - 1, :, :],
    ]
    return np.stack([plane.reshape(-1) for plane in planes]).astype(np.int32)


def ranked(outside, keys, count):
    sorting = jnp.argsort(jnp.where(outside, keys, far_away), stable=True)
    return sorting[:count]


def slot_index(local_ids, outside, count, elements):
    receivers = ranked(outside, jnp.arange(elements, dtype=jnp.int32), count)
    slots = jnp.zeros((elements,), jnp.int32).at[receivers].set(jnp.arange(count, dtype=jnp.int32))
    return jnp.where(outside, elements + slots, local_ids)


def body(state, history, inv_mass, vol_op, lift_ops, neighbors, owner):
    highest = lax.Precision.HIGHEST
    elements, width = state.shape
    table = face_table(SIDE)
    partition = lax.axis_index(("solver", "ana"))
    local = neighbors - partition * elements
    outside = (local < 0) | (local >= elements)
    span_count = LX * LY
    wall_count = LX * LZ
    counts = [0, 0, wall_count, wall_count, span_count, span_count]
    senders = [None, None] + [
        ranked(outside[face], neighbors[face], counts[face]) for face in range(2, 6)
    ]
    indices = [local[0], local[1]] + [
        slot_index(local[face], outside[face], counts[face], elements) for face in range(2, 6)
    ]
    flat_lift = lift_ops.reshape(6 * FC, width)
    ordering = jnp.argsort(owner, stable=True)
    old_rows = lax.all_to_all(
        jnp.take(history, ordering, axis=1), "ana", split_axis=1, concat_axis=1, tiled=True
    )
    field = state
    received = []
    for step in range(STEPS):
        shaped = field.reshape(elements, FIELDS, NODES)
        faces = [jnp.take(shaped, table[face], axis=2).reshape(elements, FC) for face in range(6)]
        span_out = jnp.stack(
            [jnp.take(faces[4], senders[4], axis=0), jnp.take(faces[5], senders[5], axis=0)]
        )
        span_rim = with_halo(span_out, (("solver", 0),), 1, True)
        wall_out = jnp.stack(
            [jnp.take(faces[2], senders[2], axis=0), jnp.take(faces[3], senders[3], axis=0)]
        )
        wall_rim = with_halo(wall_out, (("ana", 0),), 1, False)
        arrived = [None, None, wall_rim[0], wall_rim[3], span_rim[0], span_rim[3]]
        gathered = []
        for face in range(6):
            contact = faces[face ^ 1]
            if face >= 2:
                contact = jnp.concatenate([contact, arrived[face]], axis=0)
            gathered.append(jnp.take(contact, indices[face], axis=0))
        tendency = jnp.dot(field, vol_op, precision=highest)
        tendency = tendency + jnp.dot(
            jnp.concatenate(gathered, axis=1), flat_lift, precision=highest
        )
        applied = jnp.einsum(
            "efn,nme->efm", tendency.reshape(elements, FIELDS, NODES), inv_mass, precision=highest
        )
        field = field + time_step * applied.reshape(elements, width)
        arranged = jnp.take(field, ordering, axis=0)
        received.append(lax.all_to_all(arranged, "ana", split_axis=0, concat_axis=0, tiled=True))
    owned = jnp.stack(received)
    block = jnp.concatenate([old_rows.astype(jnp.float32), owned], axis=0).reshape(
        -1, elements * width
    )
    region_rows = elements * width * lax.axis_size("solver")
    gram = jnp.dot(block, block.T, precision=highest) / region_rows
    total = lax.psum(gram, "solver")
    lower = jnp.linalg.cholesky(total)
    upper = lower.T
    solved = lax.linalg.triangular_solve(lower, block, left_side=True, lower=True)
    return (solved.T.reshape(elements, width, -1), upper[None])


def solution(mesh):
    return jax.shard_map(
        body,
        mesh=mesh,
        in_specs=(
            P(("solver", "ana"), None),
            P(None, ("solver", "ana"), None),
            P(None, None, ("solver", "ana")),
            P(),
            P(),
            P(None, ("solver", "ana")),
            P(("solver", "ana")),
        ),
        out_specs=(P(("solver", "ana"), None, None), P("ana", None, None)),
        check_vma=False,
    )
```

profile of v0, /device:TPU:2, one launch (start us, length us, event | category | flops | bytes accessed | tf_op | source)
XLA Modules:
  0.0 469.8 jit_solution(12200236336024688298)
XLA Ops:
  29.8 4.2 collective-permute-start
  55.5 3.6 select_bitcast_fusion
  72.8 8.8 %collective-permute-start.7 = (f32[1,8,80]{2,1,0:T(8,128)S(1)}, f32[1,8,80]{2,1,0:T(8,128)S(1)}, u32[]{:S(2)}, u32[]{:S(2)}) collective-permute-start(f32[1,8,80]{2,1,0:T(8,128)S(1)} %select_bitcast_fusion.18), channel_id=1, source_target_pairs={{2,0},{4,2},{6,4},{8,6},{10,8},{12,10},{14,12},{16,14},{18,16},{20... | collective-permute-start | bytes 7688 | tf_op jit(solution)/shard_map/ppermute | solution.py:31
  85.3 13.2 %collective-permute-start.4 = (f32[1,8,80]{2,1,0:T(8,128)S(1)}, f32[1,8,80]{2,1,0:T(8,128)S(1)}, u32[]{:S(2)}, u32[]{:S(2)}) collective-permute-start(f32[1,8,80]{2,1,0:T(8,128)S(1)} %select_bitcast_fusion.21), channel_id=1, source_target_pairs={{0,1},{2,3},{4,5},{6,7},{8,9},{10,11},{12,13},{14,15},{16,17},{18,... | collective-permute-start | bytes 7688 | tf_op jit(solution)/shard_map/ppermute | solution.py:29
  111.2 7.5 %collective-permute-start.11 = (f32[1,8,80]{2,1,0:T(8,128)S(1)}, f32[1,8,80]{2,1,0:T(8,128)S(1)}, u32[]{:S(2)}, u32[]{:S(2)}) collective-permute-start(f32[1,8,80]{2,1,0:T(8,128)S(1)} %select_bitcast_fusion.14), channel_id=1, source_target_pairs={{2,0},{4,2},{6,4},{8,6},{10,8},{12,10},{14,12},{16,14},{18,16},{20... | collective-permute-start | bytes 7688 | tf_op jit(solution)/shard_map/ppermute | solution.py:31
  139.4 7.5 %collective-permute-start.15 = (f32[1,8,80]{2,1,0:T(8,128)S(1)}, f32[1,8,80]{2,1,0:T(8,128)S(1)}, u32[]{:S(2)}, u32[]{:S(2)}) collective-permute-start(f32[1,8,80]{2,1,0:T(8,128)S(1)} %select_bitcast_fusion.10), channel_id=1, source_target_pairs={{2,0},{4,2},{6,4},{8,6},{10,8},{12,10},{14,12},{16,14},{18,16},{20... | collective-permute-start | bytes 7688 | tf_op jit(solution)/shard_map/ppermute | solution.py:31
  158.3 4.4 all_to_all.41
  162.6 3.1 copy.141
  165.8 3.8 all_to_all.42
  172.6 3.8 all_to_all.43
  179.5 3.8 all_to_all.44
  183.3 3.9 all-to-all-start
  187.6 3.2 copy.144
  190.8 16.3 %concatenate.102 = f32[128,32,320]{0,2,1:T(8,128)} concatenate(bf16[124,32,320]{0,2,1:T(8,128)(2,1)S(1)} %all-to-all-done, f32[1,32,320]{0,2,1:T(8,128)} %copy.141, f32[1,32,320]{0,2,1:T(8,128)} %copy.142, f32[1,32,320]{0,2,1:T(8,128)} %copy.143, f32[1,32,320]{0,2,1:T(8,128)} %copy.144), dimensions={0} | concatenate | bytes 7946240 | tf_op jit(solution)/shard_map/concatenate | solution.py:114
  207.1 13.1 %fusion = f32[128,128]{0,1:T(8,128)} fusion(f32[128,32,320]{0,2,1:T(8,128)} %concatenate.102), kind=kOutput, calls=%fused_computation.79 | convolution fusion | flops 2013282304 | bytes 5308416 | tf_op jit(solution)/shard_map/dot_general | solution.py:118
  223.2 6.6 %concatenate.103 = f32[1,10240]{0,1:T(8,128)} reshape(f32[2,16,320]{2,1,0:T(8,128)S(1)} %all_to_all.41) | data formatting | bytes 81920 | tf_op jit(solution)/shard_map/concatenate | solution.py:114
  229.7 6.6 %concatenate.104 = f32[1,10240]{0,1:T(8,128)} reshape(f32[2,16,320]{2,1,0:T(8,128)S(1)} %all_to_all.42) | data formatting | bytes 81920 | tf_op jit(solution)/shard_map/concatenate | solution.py:114
  236.4 6.4 %concatenate.105 = f32[1,10240]{0,1:T(8,128)} reshape(f32[2,16,320]{2,1,0:T(8,128)S(1)} %all_to_all.43) | data formatting | bytes 81920 | tf_op jit(solution)/shard_map/concatenate | solution.py:114
  242.8 6.5 %concatenate.106 = f32[1,10240]{0,1:T(8,128)} reshape(f32[2,16,320]{2,1,0:T(8,128)S(1)} %all_to_all.44) | data formatting | bytes 81920 | tf_op jit(solution)/shard_map/concatenate | solution.py:114
  249.4 17.3 %concatenate.101 = f32[128,10240]{0,1:T(8,128)} concatenate(f32[124,10240]{0,1:T(8,128)} %bitcast.216, f32[1,10240]{0,1:T(8,128)} %concatenate.103, f32[1,10240]{0,1:T(8,128)} %concatenate.104, f32[1,10240]{0,1:T(8,128)} %concatenate.105, f32[1,10240]{0,1:T(8,128)} %concatenate.106), dimensions={0} | concatenate | bytes 10485760 | tf_op jit(solution)/shard_map/concatenate | solution.py:114
  266.6 162.9 %all-reduce.2.cloned.1.call-done = f32[128,128]{0,1:T(8,128)} async-done(((f32[128,128]{0,1:T(8,128)}), f32[128,128]{0,1:T(8,128)}) %all-reduce.2.cloned.1.call-update) | async-done | bytes 65552 | tf_op jit(solution)/shard_map/psum | solution.py:119
  431.3 11.7 %cholesky.16 = f32[128,128]{1,0:T(8,128)S(1)} custom-call(f32[128,128]{1,0:T(8,128)S(1)} %fusion.7), custom_call_target="Cholesky" | custom-call | tf_op jit(solution)/shard_map/jit(cholesky)/cholesky | solution.py:120
  444.4 9.8 %custom-call.6 = f32[1,128,128]{1,2,0:T(8,128)S(1)} custom-call(f32[1,128,128]{2,1,0:T(8,128)S(1)} %get-tuple-element.52), custom_call_target="InvertDiagBlocksLowerTriangular" | custom-call | tf_op jit(solution)/shard_map/triangular_solve | solution.py:122
  454.9 7.8 %fusion.5 = f32[32,320,128]{2,1,0:T(8,128)} fusion(f32[32,320,128]{2,1,0:T(8,128)} %bitcast.215, f32[1,128,128]{1,2,0:T(8,128)S(1)} %custom-call.6), kind=kOutput, calls=%fused_computation.88 | convolution fusion | flops 2013265920 | bytes 10551296 | tf_op jit(solution)/shard_map/triangular_solve | solution.py:122
  (374 shorter events, 118.6 us)
Async XLA Ops:
  7.2 45.9 %copy-start = (bf16[124,32,320]{0,2,1:T(8,128)(2,1)S(1)}, bf16[124,32,320]{0,2,1:T(8,128)(2,1)}, u32[]{:S(2)}) copy-start(bf16[124,32,320]{0,2,1:T(8,128)(2,1)} %param.42) | copy-start | bytes 7618564
  13.6 45.6 %collective-permute-start.3 = (f32[1,8,80]{2,1,0:T(8,128)}, f32[1,8,80]{2,1,0:T(8,128)}, u32[]{:S(2)}, u32[]{:S(2)}) collective-permute-start(f32[1,8,80]{2,1,0:T(8,128)} %select_bitcast_fusion.22), channel_id=1, source_target_pairs={{2,0},{4,2},{6,4},{8,6},{10,8},{12,10},{14,12},{16,14},{18,16},{20... | collective-permute-start | bytes 7688 | tf_op jit(solution)/shard_map/ppermute | solution.py:31
  20.1 39.8 %collective-permute-start.2 = (f32[1,8,80]{2,1,0:T(8,128)}, f32[1,8,80]{2,1,0:T(8,128)}, u32[]{:S(2)}, u32[]{:S(2)}) collective-permute-start(f32[1,8,80]{2,1,0:T(8,128)} %select_bitcast_fusion.23), channel_id=1, source_target_pairs={{0,2},{2,4},{4,6},{6,8},{8,10},{10,12},{12,14},{14,16},{16,18},{18... | collective-permute-start | bytes 7688 | tf_op jit(solution)/shard_map/ppermute | solution.py:29
  24.3 36.3 %collective-permute-start.1 = (f32[1,8,80]{2,1,0:T(8,128)}, f32[1,8,80]{2,1,0:T(8,128)}, u32[]{:S(2)}, u32[]{:S(2)}) collective-permute-start(f32[1,8,80]{2,1,0:T(8,128)} %select_bitcast_fusion.24), channel_id=1, source_target_pairs={{1,0},{3,2},{5,4},{7,6},{9,8},{11,10},{13,12},{15,14},{17,16},{19,... | collective-permute-start | bytes 7688 | tf_op jit(solution)/shard_map/ppermute | solution.py:31
  29.8 31.5 %collective-permute-start = (f32[1,8,80]{2,1,0:T(8,128)}, f32[1,8,80]{2,1,0:T(8,128)}, u32[]{:S(2)}, u32[]{:S(2)}) collective-permute-start(f32[1,8,80]{2,1,0:T(8,128)} %select_bitcast_fusion.25), channel_id=1, source_target_pairs={{0,1},{2,3},{4,5},{6,7},{8,9},{10,11},{12,13},{14,15},{16,17},{18,... | collective-permute-start | bytes 7688 | tf_op jit(solution)/shard_map/ppermute | solution.py:29
  55.5 26.7 %copy-start.25 = (pred[8]{0:T(512)(128)(4,1)S(1)}, pred[8]{0:T(512)(128)(4,1)}, u32[]{:S(2)}) copy-start(pred[8]{0:T(512)(128)(4,1)} %copy-done.24) | copy-start | bytes 28
  55.5 27.5 %copy-start.23 = (pred[8]{0:T(512)(128)(4,1)S(1)}, pred[8]{0:T(512)(128)(4,1)}, u32[]{:S(2)}) copy-start(pred[8]{0:T(512)(128)(4,1)} %copy-done.22) | copy-start | bytes 28
  59.2 26.0 %copy-start.27 = (pred[8]{0:T(512)(128)(4,1)S(1)}, pred[8]{0:T(512)(128)(4,1)}, u32[]{:S(2)}) copy-start(pred[8]{0:T(512)(128)(4,1)} %copy-done.26) | copy-start | bytes 28
  59.2 39.3 %copy-start.19 = (pred[16]{0:T(512)(128)(4,1)S(1)}, pred[16]{0:T(512)(128)(4,1)}, u32[]{:S(2)}) copy-start(pred[16]{0:T(512)(128)(4,1)} %copy-done.18) | copy-start | bytes 52
  72.8 27.4 %collective-permute-start.7 = (f32[1,8,80]{2,1,0:T(8,128)S(1)}, f32[1,8,80]{2,1,0:T(8,128)S(1)}, u32[]{:S(2)}, u32[]{:S(2)}) collective-permute-start(f32[1,8,80]{2,1,0:T(8,128)S(1)} %select_bitcast_fusion.18), channel_id=1, source_target_pairs={{2,0},{4,2},{6,4},{8,6},{10,8},{12,10},{14,12},{16,14},{18,16},{20... | collective-permute-start | bytes 7688 | tf_op jit(solution)/shard_map/ppermute | solution.py:31
  82.3 18.6 %collective-permute-start.6 = (f32[1,8,80]{2,1,0:T(8,128)S(1)}, f32[1,8,80]{2,1,0:T(8,128)S(1)}, u32[]{:S(2)}, u32[]{:S(2)}) collective-permute-start(f32[1,8,80]{2,1,0:T(8,128)S(1)} %select_bitcast_fusion.19), channel_id=1, source_target_pairs={{0,2},{2,4},{4,6},{6,8},{8,10},{10,12},{12,14},{14,16},{16,18},{18... | collective-permute-start | bytes 7688 | tf_op jit(solution)/shard_map/ppermute | solution.py:29
  83.1 18.5 %collective-permute-start.5 = (f32[1,8,80]{2,1,0:T(8,128)S(1)}, f32[1,8,80]{2,1,0:T(8,128)S(1)}, u32[]{:S(2)}, u32[]{:S(2)}) collective-permute-start(f32[1,8,80]{2,1,0:T(8,128)S(1)} %select_bitcast_fusion.20), channel_id=1, source_target_pairs={{1,0},{3,2},{5,4},{7,6},{9,8},{11,10},{13,12},{15,14},{17,16},{19,... | collective-permute-start | bytes 7688 | tf_op jit(solution)/shard_map/ppermute | solution.py:31
  85.3 17.0 %collective-permute-start.4 = (f32[1,8,80]{2,1,0:T(8,128)S(1)}, f32[1,8,80]{2,1,0:T(8,128)S(1)}, u32[]{:S(2)}, u32[]{:S(2)}) collective-permute-start(f32[1,8,80]{2,1,0:T(8,128)S(1)} %select_bitcast_fusion.21), channel_id=1, source_target_pairs={{0,1},{2,3},{4,5},{6,7},{8,9},{10,11},{12,13},{14,15},{16,17},{18,... | collective-permute-start | bytes 7688 | tf_op jit(solution)/shard_map/ppermute | solution.py:29
  111.2 15.9 %collective-permute-start.11 = (f32[1,8,80]{2,1,0:T(8,128)S(1)}, f32[1,8,80]{2,1,0:T(8,128)S(1)}, u32[]{:S(2)}, u32[]{:S(2)}) collective-permute-start(f32[1,8,80]{2,1,0:T(8,128)S(1)} %select_bitcast_fusion.14), channel_id=1, source_target_pairs={{2,0},{4,2},{6,4},{8,6},{10,8},{12,10},{14,12},{16,14},{18,16},{20... | collective-permute-start | bytes 7688 | tf_op jit(solution)/shard_map/ppermute | solution.py:31
  119.3 9.0 %collective-permute-start.10 = (f32[1,8,80]{2,1,0:T(8,128)S(1)}, f32[1,8,80]{2,1,0:T(8,128)S(1)}, u32[]{:S(2)}, u32[]{:S(2)}) collective-permute-start(f32[1,8,80]{2,1,0:T(8,128)S(1)} %select_bitcast_fusion.15), channel_id=1, source_target_pairs={{0,2},{2,4},{4,6},{6,8},{8,10},{10,12},{12,14},{14,16},{16,18},{18... | collective-permute-start | bytes 7688 | tf_op jit(solution)/shard_map/ppermute | solution.py:29
  120.1 8.9 %collective-permute-start.9 = (f32[1,8,80]{2,1,0:T(8,128)S(1)}, f32[1,8,80]{2,1,0:T(8,128)S(1)}, u32[]{:S(2)}, u32[]{:S(2)}) collective-permute-start(f32[1,8,80]{2,1,0:T(8,128)S(1)} %select_bitcast_fusion.16), channel_id=1, source_target_pairs={{1,0},{3,2},{5,4},{7,6},{9,8},{11,10},{13,12},{15,14},{17,16},{19,... | collective-permute-start | bytes 7688 | tf_op jit(solution)/shard_map/ppermute | solution.py:31
  122.2 7.5 %collective-permute-start.8 = (f32[1,8,80]{2,1,0:T(8,128)S(1)}, f32[1,8,80]{2,1,0:T(8,128)S(1)}, u32[]{:S(2)}, u32[]{:S(2)}) collective-permute-start(f32[1,8,80]{2,1,0:T(8,128)S(1)} %select_bitcast_fusion.17), channel_id=1, source_target_pairs={{0,1},{2,3},{4,5},{6,7},{8,9},{10,11},{12,13},{14,15},{16,17},{18,... | collective-permute-start | bytes 7688 | tf_op jit(solution)/shard_map/ppermute | solution.py:29
  131.1 27.1 %copy-start.29 = (pred[32]{0:T(512)(128)(4,1)S(1)}, pred[32]{0:T(512)(128)(4,1)}, u32[]{:S(2)}) copy-start(pred[32]{0:T(512)(128)(4,1)} %compare_and_fusion.11) | copy-start | bytes 100
  138.5 14.2 %collective-permute-start.14 = (f32[1,8,80]{2,1,0:T(8,128)S(1)}, f32[1,8,80]{2,1,0:T(8,128)S(1)}, u32[]{:S(2)}, u32[]{:S(2)}) collective-permute-start(f32[1,8,80]{2,1,0:T(8,128)S(1)} %select_bitcast_fusion.11), channel_id=1, source_target_pairs={{0,2},{2,4},{4,6},{6,8},{8,10},{10,12},{12,14},{14,16},{16,18},{18... | collective-permute-start | bytes 7688 | tf_op jit(solution)/shard_map/ppermute | solution.py:29
  139.4 13.4 %collective-permute-start.15 = (f32[1,8,80]{2,1,0:T(8,128)S(1)}, f32[1,8,80]{2,1,0:T(8,128)S(1)}, u32[]{:S(2)}, u32[]{:S(2)}) collective-permute-start(f32[1,8,80]{2,1,0:T(8,128)S(1)} %select_bitcast_fusion.10), channel_id=1, source_target_pairs={{2,0},{4,2},{6,4},{8,6},{10,8},{12,10},{14,12},{16,14},{18,16},{20... | collective-permute-start | bytes 7688 | tf_op jit(solution)/shard_map/ppermute | solution.py:31
  147.7 5.1 %collective-permute-start.12 = (f32[1,8,80]{2,1,0:T(8,128)S(1)}, f32[1,8,80]{2,1,0:T(8,128)S(1)}, u32[]{:S(2)}, u32[]{:S(2)}) collective-permute-start(f32[1,8,80]{2,1,0:T(8,128)S(1)} %select_bitcast_fusion.13), channel_id=1, source_target_pairs={{0,1},{2,3},{4,5},{6,7},{8,9},{10,11},{12,13},{14,15},{16,17},{18,... | collective-permute-start | bytes 7688 | tf_op jit(solution)/shard_map/ppermute | solution.py:29
  151.4 3.1 collective-permute-start.13
  183.3 7.5 %all-to-all-start = ((bf16[124,32,320]{0,2,1:T(8,128)(2,1)}), bf16[124,32,320]{0,2,1:T(8,128)(2,1)S(1)}, u32[]{:S(2)}, u32[]{:S(2)}) async-start(bf16[124,32,320]{0,2,1:T(8,128)(2,1)} %select_bitcast_fusion), calls=%async_computation | async-start | bytes 5242880 | tf_op jit(solution)/shard_map/all_to_all | solution.py:80
  187.2 242.4 %all-reduce.2.cloned.1.call-start = ((), (), s32[]{:S(2)}) async-start(), calls=%async_computation.5 | async-start | bytes 131072 | tf_op jit(solution)/shard_map/psum | solution.py:119
  (24 other events, 223.8 us)
Sparse Core Ops, SparseCore 0:
  220.3 209.1 all-reduce.1
where the time goes:
time: 479 us; the launch traced here: 470 us
  waiting for transfers between devices  164 us (34%)
  local copies, waits for them, and re-layouts  125 us (26%)
  other arithmetic  61.5 us (13%)
  starting transfers between devices  57.1 us (12%)
  matrix products  31.4 us (7%)
  blocking collectives  15.7 us (3%)
  between operations  15.6 us (3%)
    psum x1, waiting for transfers between devices, body(): total = lax.psum(gram, 'solver')  163 us
    concatenate x6, local copies, waits for them, and re-layouts, body(): jnp.concatenate([old_rows.astype(jnp.float32), owned], axis=0)  59.8 us
    ppermute x8, starting transfers between devices, with_halo(): lax.ppermute(head, axis, [((i + 1) % count, i) for i in range(ends)])  31.1 us
    ppermute x8, starting transfers between devices, with_halo(): lax.ppermute(tail, axis, [(i, (i + 1) % count) for i in range(ends)])  21.7 us
    all_to_all x4, blocking collectives, body(): lax.all_to_all(arranged, 'ana', split_axis=0, concat_axis=0, tiled=True)  15.7 us
    gather x40, local copies, waits for them, and re-layouts, body(): jnp.take(shaped, table[face], axis=2).reshape(elements, FC)  15.2 us
    gather x24, local copies, waits for them, and re-layouts, body(): gathered.append(jnp.take(contact, indices[face], axis=0))  14.6 us
    dot_general x1, matrix products, body(): gram = jnp.dot(block, block.T, precision=highest) / region_rows  13.1 us
  transfers between devices with their start and end apart: 18, of which 2 were waited for; matrix products, arithmetic and copies ran while one was open for 23% of the time, Pallas kernels for 0%

commit v1 on v0

v1 whole, which is shorter than its diff:
```python
import functools

import jax
import jax.numpy as jnp
from jax import lax
from jax.experimental import pallas as pl
from jax.experimental.pallas import tpu as pltpu
from jax.sharding import PartitionSpec as P

F32 = jnp.float32
BF16 = jnp.bfloat16
I32 = jnp.int32
HIGHEST = lax.Precision.HIGHEST

EL = 32
HALF = 16
C = 320
CP = 384
NODES = 64
HIST = 124
SNAPS = 128
STEPS = 4
RIM = 8
time_step = 0.2


def iota(shape, dim):
    return lax.broadcasted_iota(I32, shape, dim)


def mm(a, b):
    return jnp.dot(a, b, preferred_element_type=F32)


def split2(x):
    high = x.astype(BF16)
    return high, (x - high.astype(F32)).astype(BF16)


def contacts(field, sel):
    high, low = split2(field)
    out = mm(jnp.concatenate([high, low], axis=0), sel)
    return out[:EL].astype(BF16), out[EL:].astype(BF16)


def send_faces(snd, chi, clo):
    out = mm(snd, chi[:, 256:768]) + mm(snd, clo[:, 256:768])
    return (
        out[0:8, 384:512],
        out[8:16, 256:384],
        out[16:24, 128:256] + out[24:32, 0:128],
    )


def setup_kernel(base_ref, nbr_any, own_any, state_any, gd_ref, snd_ref, order_ref, sel_ref, chi_ref, clo_ref, zdn_ref, zup_ref, y_ref, nbr_ref, own_ref, state_ref, sem):
    copies = [
        pltpu.make_async_copy(src, dst, sem.at[k])
        for k, (src, dst) in enumerate(((nbr_any, nbr_ref), (own_any, own_ref), (state_any, state_ref)))
    ]
    for copy in copies:
        copy.start()
    for copy in copies:
        copy.wait()
    base = base_ref[0]
    sub = iota((EL, EL), 0)
    lane = iota((EL, EL), 1)
    eye = sub == lane

    def column(row):
        return jnp.sum(jnp.where(eye, jnp.broadcast_to(row, (EL, EL)), 0), axis=1, keepdims=True)

    sends = {}
    for face in range(6):
        row = nbr_ref[face : face + 1, :]
        col = column(row)
        local = col - base
        g = jnp.where(local == lane, 1.0, 0.0)
        if face >= 2:
            out_row = jnp.where((row >= 0) & ((row < base) | (row >= base + EL)), 1, 0)
            out_col = column(out_row)
            rank_out = jnp.sum(jnp.where((out_col > 0) & (col < row), 1, 0), axis=0, keepdims=True)
            s = (rank_out == iota((RIM, EL), 0)) & (out_row > 0)
            sends[face] = jnp.where(s, 1.0, 0.0)
            rank_in = jnp.sum(jnp.where((out_row > 0) & (lane < sub), 1, 0), axis=1, keepdims=True)
            d = (rank_in == iota((EL, 16), 1)) & (out_col > 0)
            d = jnp.where(d, 1.0, 0.0)
        else:
            d = jnp.zeros((EL, 16), F32)
        gd_ref[face] = jnp.concatenate([g, d], axis=1).astype(BF16)
    snd = jnp.concatenate([sends[4], sends[5], sends[2], sends[3]], axis=0).astype(BF16)
    snd_ref[...] = snd
    own_row = own_ref[...]
    own_col = column(own_row)
    rank = jnp.sum(jnp.where((own_col == own_row) & (sub < lane), 1, 0), axis=0, keepdims=True) + HALF * own_row
    rank_col = column(rank)
    order_ref[...] = jnp.sum(jnp.where(rank_col == lane, sub, 0), axis=0, keepdims=True)
    col = iota((1, 768), 1)
    face = col // 128
    rest = col % 128
    var = rest // 16
    q = rest % 16
    slow = q // 4
    fast = q % 4
    axis = face // 2
    side = 3 * (1 - face % 2)
    node = jnp.where(
        axis == 0,
        side + 4 * fast + 16 * slow,
        jnp.where(axis == 1, fast + 4 * side + 16 * slow, fast + 4 * slow + 16 * side),
    )
    target = jnp.where(rest < 80, var * NODES + node, -1)
    sel = jnp.where(iota((C, 768), 0) == target, 1.0, 0.0).astype(BF16)
    sel_ref[...] = sel
    chi, clo = contacts(state_ref[...], sel)
    chi_ref[...] = chi
    clo_ref[...] = clo
    zdn_ref[...], zup_ref[...], y_ref[...] = send_faces(snd, chi, clo)


def prep_kernel(vol_ref, lift_ref, mass_ref, w_ref, m_ref):
    w_ref[...] = jnp.zeros_like(w_ref)
    high, low = split2(vol_ref[...])
    w_ref[0:C, 0:C] = high
    w_ref[0:C, CP : CP + C] = low
    for face in range(6):
        high, low = split2(lift_ref[face])
        start = CP + 128 * face
        w_ref[start : start + 80, 0:C] = high
        w_ref[start : start + 80, CP : CP + C] = low
    high, low = split2(mass_ref[...])
    m_ref[:, 0:NODES] = high
    m_ref[:, NODES:128] = low


def step_kernel(last, order_ref, ana_ref, field_ref, chi_ref, clo_ref, gd_ref, snd_ref, sel_ref, w_ref, m_ref, zlo_ref, zhi_ref, y_ref, *outs):
    rest = list(outs)
    new_ref = rest.pop() if last else rest.pop(0)
    field = field_ref[...]
    fhi, flo = split2(field)
    pad = jnp.zeros((EL, CP - C), BF16)
    his = [fhi, pad]
    los = [flo, pad]
    y_in = y_ref[0:RIM, 0:128]
    arrived = {2: y_in, 3: y_in, 4: zlo_ref[...], 5: zhi_ref[...]}
    for face in range(6):
        lanes = slice(128 * face, 128 * face + 128)
        rows = jnp.concatenate([chi_ref[:, lanes], clo_ref[:, lanes]], axis=1)
        if face >= 2:
            ahi, alo = split2(jnp.concatenate([arrived[face], jnp.zeros((8, 128), F32)], axis=0))
            rows = jnp.concatenate([rows, jnp.concatenate([ahi, alo], axis=1)], axis=0)
            picked = mm(gd_ref[face], rows)
        else:
            picked = mm(gd_ref[face, :, 0:EL], rows)
        his.append(picked[:, 0:128].astype(BF16))
        los.append(picked[:, 128:256].astype(BF16))
    both = jnp.concatenate([jnp.concatenate(his, axis=1), jnp.concatenate(los, axis=1)], axis=0)
    prod = mm(both, w_ref[...])
    tend = (prod[:EL, 0:C] + prod[EL:, 0:C]) + (prod[:EL, CP : CP + C] + prod[EL:, CP : CP + C])
    own_block = iota((HALF, 1024), 1) // NODES == iota((HALF, 1024), 0)
    parts = []
    for tile in range(2):
        his = []
        los = []
        for var in range(5):
            one = tend[HALF * tile : HALF * tile + HALF, NODES * var : NODES * var + NODES]
            wide = jnp.concatenate([one, one], axis=1)
            wide = jnp.concatenate([wide] * 8, axis=1)
            high, low = split2(jnp.where(own_block, wide, 0.0))
            his.append(high)
            los.append(low)
        left = jnp.concatenate(his + los, axis=0)
        prod = mm(left, m_ref[1024 * tile : 1024 * tile + 1024, :])
        prod = prod[0:80] + prod[80:160]
        prod = prod[:, 0:NODES] + prod[:, NODES:128]
        parts.append(jnp.concatenate([prod[HALF * var : HALF * var + HALF] for var in range(5)], axis=1))
    new = field + time_step * jnp.concatenate(parts, axis=0)
    new_ref[...] = new
    ana = ana_ref[0]
    if last:
        fown_ref, fsend_ref = rest
        first = 0
    else:
        chi_out, clo_out, zdn_ref, zup_ref, fsend_ref, fown_ref = rest
        first = RIM
        chi, clo = contacts(new, sel_ref[...])
        chi_out[...] = chi
        clo_out[...] = clo
        zdn, zup, y = send_faces(snd_ref[...], chi, clo)
        zdn_ref[...] = zdn
        zup_ref[...] = zup
        fsend_ref[0:RIM, 0:128] = y
        fsend_ref[0:RIM, 128:CP] = jnp.zeros((RIM, CP - 128), F32)
    fsend_ref[first : first + HALF, C:CP] = jnp.zeros((HALF, CP - C), F32)
    fown_ref[:, C:CP] = jnp.zeros((HALF, CP - C), F32)
    for k in range(HALF):
        mine = order_ref[0, ana * HALF + k]
        other = order_ref[0, (1 - ana) * HALF + k]
        fown_ref[k : k + 1, 0:C] = new_ref[pl.ds(mine, 1), :]
        fsend_ref[first + k : first + k + 1, 0:C] = new_ref[pl.ds(other, 1), :]


def pick_kernel(order_ref, ana_ref, hist_ref, keep_ref, sent_ref, sem):
    ana = ana_ref[0]
    copies = []
    for k in range(HALF):
        copies.append(pltpu.make_async_copy(hist_ref.at[order_ref[0, ana * HALF + k]], keep_ref.at[k], sem.at[k]))
        copies.append(
            pltpu.make_async_copy(hist_ref.at[order_ref[0, (1 - ana) * HALF + k]], sent_ref.at[k], sem.at[HALF + k])
        )
    for copy in copies:
        copy.start()
    for copy in copies:
        copy.wait()


def gram_kernel(keep_ref, sent_ref, mine_ref, theirs_ref):
    for ref, out_ref in ((keep_ref, mine_ref), (sent_ref, theirs_ref)):
        total = None
        for k in range(0, HALF, 4):
            rows = ref[k : k + 4].reshape(4 * C, HIST)
            part = lax.dot_general(rows, rows, (((0,), (0,)), ((), ())), preferred_element_type=F32)
            total = part if total is None else total + part
        out_ref[...] = jnp.zeros_like(out_ref)
        out_ref[0:HIST, 0:HIST] = total


def factor_kernel(scale, gram_ref, up_ref, inv_ref):
    tiles = SNAPS // 8
    row = iota((SNAPS, SNAPS), 0)
    col = iota((SNAPS, SNAPS), 1)
    start = jnp.where((row < HIST) & (col < HIST), gram_ref[...] * scale, jnp.where(row == col, 1.0, 0.0))
    ident = jnp.where(row == col, 1.0, 0.0)
    a = [start[8 * t : 8 * t + 8] for t in range(tiles)]
    b = [ident[8 * t : 8 * t + 8] for t in range(tiles)]
    below = iota((8, SNAPS), 0)
    for j in range(0, HIST, 2):
        t = j // 8
        r = j % 8
        a0 = a[t][r : r + 1, :]
        a1 = a[t][r + 1 : r + 2, :]
        b0 = b[t][r : r + 1, :]
        b1 = b[t][r + 1 : r + 2, :]
        p = a0[:, j : j + 1]
        q = a0[:, j + 1 : j + 2]
        s = a1[:, j + 1 : j + 2]
        inv = 1.0 / (p * s - q * q)
        ip = jnp.broadcast_to(s * inv, (1, SNAPS))
        iq = jnp.broadcast_to(q * inv, (1, SNAPS))
        js = jnp.broadcast_to(p * inv, (1, SNAPS))
        sa0 = jnp.broadcast_to(ip * a0 - iq * a1, (8, SNAPS))
        sa1 = jnp.broadcast_to(js * a1 - iq * a0, (8, SNAPS))
        sb0 = jnp.broadcast_to(ip * b0 - iq * b1, (8, SNAPS))
        sb1 = jnp.broadcast_to(js * b1 - iq * b0, (8, SNAPS))
        for k in range(t, tiles):
            if k == t and r == 6:
                continue
            m0 = jnp.broadcast_to(a[k][:, j : j + 1], (8, SNAPS))
            m1 = jnp.broadcast_to(a[k][:, j + 1 : j + 2], (8, SNAPS))
            if k == t:
                m0 = jnp.where(below > r + 1, m0, 0.0)
                m1 = jnp.where(below > r + 1, m1, 0.0)
            a[k] = a[k] - m0 * sa0 - m1 * sa1
            b[k] = b[k] - m0 * sb0 - m1 * sb1
    up = jnp.concatenate(a, axis=0)
    low = jnp.concatenate(b, axis=0)
    odd = (iota((SNAPS, 1), 0) % 2) == 1
    diag = jnp.sum(jnp.where(row == col, up, 0.0), axis=1, keepdims=True)
    side = jnp.sum(jnp.where(row == col + 1, up, 0.0), axis=1, keepdims=True)
    before = pltpu.roll(jnp.broadcast_to(diag, (SNAPS, SNAPS)), 1, 0)[:, 0:1]
    ratio = jnp.where(odd, side / before, 0.0)
    root = 1.0 / jnp.sqrt(diag - ratio * side)
    up = (up - ratio * pltpu.roll(up, 1, 0)) * root
    low = (low - ratio * pltpu.roll(low, 1, 0)) * root
    up_ref[...] = jnp.where(col >= row, up, 0.0)
    inv_ref[...] = jnp.where(col <= row, low, 0.0)


def rows_kernel(fields_ref, keep_ref, other_ref, out_ref, turned_ref):
    f = fields_ref[...]
    high = f.astype(BF16).astype(F32)
    mid = (f - high).astype(BF16).astype(F32)
    low = f - high - mid
    zero = jnp.zeros((4, C), F32)
    total = None
    for half, ref in ((0, keep_ref), (1, other_ref)):
        for k in range(HALF):
            at = slice(64 * half + 4 * k, 64 * half + 4 * k + 4)
            left = jnp.concatenate([high[at, 0:C], mid[at, 0:C], low[at, 0:C], zero], axis=0).astype(BF16)
            part = mm(left, ref[k])
            total = part if total is None else total + part
    rows = total[0:4] + total[4:8] + total[8:12]
    rows = jnp.concatenate([rows, jnp.zeros((4, 4), F32)], axis=1)
    lane = iota((4, SNAPS), 1)
    sub = iota((4, SNAPS), 0)
    for d in range(STEPS):
        other = f if d == 0 else pltpu.roll(f, SNAPS - d, 0)
        pair = jnp.sum(f * other, axis=1, keepdims=True)
        for s in range(STEPS - d):
            both = jnp.sum(jnp.where(iota((SNAPS, 1), 0) % 4 == s, pair, 0.0), axis=0, keepdims=True)
            at = (sub == s) & (lane == HIST + s + d)
            at = at | ((sub == s + d) & (lane == HIST + s))
            rows = jnp.where(at, both, rows)
    out_ref[...] = jnp.broadcast_to(rows[None], out_ref.shape)
    turned = f.T[0:C]
    high, low = split2(turned)
    turned_ref[:, 0:SNAPS] = high
    turned_ref[:, SNAPS : 2 * SNAPS] = low


def border_kernel(scale, gathered_ref, up_ref, inv_ref, w_ref, wf_ref, fac_ref):
    rows = jnp.sum(gathered_ref[...], axis=0) * scale
    lane = iota((4, SNAPS), 1)
    g21 = jnp.where(lane < HIST, rows, 0.0)
    inv = inv_ref[...]
    l21 = lax.dot_general(g21, inv, (((1,), (1,)), ((), ())), precision=HIGHEST, preferred_element_type=F32)
    l21 = jnp.where(lane < HIST, l21, 0.0)
    comp = [[None] * 4 for _ in range(4)]
    for s in range(4):
        for u in range(s, 4):
            g = jnp.sum(jnp.where(lane[0:1] == HIST + u, rows[s : s + 1], 0.0), axis=1, keepdims=True)
            comp[s][u] = g - jnp.sum(l21[s : s + 1] * l21[u : u + 1], axis=1, keepdims=True)
    tail = lax.dot_general(l21, inv, (((1,), (0,)), ((), ())), precision=HIGHEST, preferred_element_type=F32)
    unit = jnp.where(lane == iota((4, SNAPS), 0) + HIST, 1.0, 0.0)
    work = [unit[s : s + 1] - tail[s : s + 1] for s in range(4)]
    ups = []
    outs = []
    for s in range(4):
        root = 1.0 / jnp.sqrt(comp[s][s])
        urow = [None] * 4
        for u in range(s, 4):
            urow[u] = comp[s][u] * root
        ups.append(urow)
        outs.append(work[s] * root)
        for u in range(s + 1, 4):
            work[u] = work[u] - urow[u] * outs[s]
            for v in range(u, 4):
                comp[u][v] = comp[u][v] - urow[u] * urow[v]
    new_rows = jnp.concatenate(outs, axis=0)
    full = jnp.concatenate([inv[0:HIST], new_rows], axis=0)
    wide = full.T
    high, low = split2(wide)
    w_ref[:, 0:SNAPS] = high
    w_ref[:, SNAPS : 2 * SNAPS] = low
    ends = jnp.concatenate([high[HIST:], low[HIST:]], axis=1).astype(F32)
    ends = jnp.concatenate([ends, ends], axis=0)
    wf_ref[...] = jnp.concatenate([ends] * 32, axis=0).astype(BF16)
    tri = jnp.zeros((4, SNAPS), F32)
    sub = iota((4, SNAPS), 0)
    for s in range(4):
        for u in range(s, 4):
            tri = jnp.where((sub == s) & (lane == HIST + u), ups[s][u], tri)
    lower = up_ref[...].T
    lower = jnp.concatenate([lower[0:HIST], l21], axis=0)
    upper = lower.T
    fac_ref[0] = jnp.concatenate([upper[0:HIST], tri], axis=0)


def final_kernel(ana_ref, w_ref, wf_ref, turned_ref, keep_ref, other_ref, out_ref):
    i = pl.program_id(0)
    ana = ana_ref[0]
    main = w_ref[0:HIST, :]
    ends = wf_ref[...].astype(F32)
    turned = turned_ref[...]
    element = (iota((2 * SNAPS, 2 * SNAPS), 0) % SNAPS) // 4
    for half, which, ref in ((0, ana, keep_ref), (1, 1 - ana, other_ref)):
        for k in range(2):
            at = 2 * i + k
            tail = jnp.where(element == at + HALF * half, ends, 0.0).astype(BF16)
            prod = mm(ref[at], main) + mm(turned, tail)
            out_ref[which, k] = prod[:, 0:SNAPS] + prod[:, SNAPS : 2 * SNAPS]


def shape(dims, kind=F32):
    return jax.ShapeDtypeStruct(dims, kind)


SMEM = pl.BlockSpec(memory_space=pltpu.SMEM)
VMEM = pl.BlockSpec(memory_space=pltpu.VMEM)
ANY = pl.BlockSpec(memory_space=pl.ANY)
PARAMS = pltpu.CompilerParams(vmem_limit_bytes=40 << 20)


def body(state, history, inv_mass, vol_op, lift_ops, neighbors, owner):
    groups = lax.axis_size("solver")
    ana = lax.axis_index("ana").astype(I32)
    base = (lax.axis_index(("solver", "ana")) * EL).astype(I32).reshape(1)
    ana = ana.reshape(1)
    hist = jnp.transpose(history, (1, 2, 0))
    mass = jnp.transpose(inv_mass, (2, 0, 1)).reshape(EL * NODES, NODES)
    scale = 1.0 / (EL * C * groups)
    rise = [(i, (i + 1) % groups) for i in range(groups)]
    fall = [((i + 1) % groups, i) for i in range(groups)]
    swap = [(0, 1), (1, 0)]

    gd, snd, order, sel, chi, clo, zdn, zup, yout = pl.pallas_call(
        setup_kernel,
        in_specs=[SMEM, ANY, ANY, ANY],
        scratch_shapes=[
            pltpu.VMEM((6, EL), I32),
            pltpu.VMEM((1, EL), I32),
            pltpu.VMEM((EL, C), F32),
            pltpu.SemaphoreType.DMA((3,)),
        ],
        out_shape=(
            shape((6, EL, 48), BF16),
            shape((EL, EL), BF16),
            shape((1, EL), I32),
            shape((C, 768), BF16),
            shape((EL, 768), BF16),
            shape((EL, 768), BF16),
            shape((RIM, 128)),
            shape((RIM, 128)),
            shape((RIM, 128)),
        ),
        compiler_params=PARAMS,
        name="setup",
    )(base, neighbors, owner.reshape(1, EL), state)

    keep, sent = pl.pallas_call(
        pick_kernel,
        in_specs=[SMEM, SMEM, ANY],
        out_shape=(shape((HALF, C, HIST), BF16), shape((HALF, C, HIST), BF16)),
        scratch_shapes=[pltpu.SemaphoreType.DMA((2 * HALF,))],
        compiler_params=PARAMS,
        name="pick",
    )(order, ana, hist)
    other = lax.ppermute(sent, "ana", swap)

    w, m = pl.pallas_call(
        prep_kernel,
        in_specs=[VMEM, VMEM, VMEM],
        out_shape=(shape((CP + 768, 2 * CP), BF16), shape((EL * NODES, 128), BF16)),
        compiler_params=PARAMS,
        name="prep",
    )(vol_op, lift_ops, mass)

    gram, theirs = pl.pallas_call(
        gram_kernel,
        in_specs=[VMEM, VMEM],
        out_shape=(shape((SNAPS, SNAPS)), shape((SNAPS, SNAPS))),
        compiler_params=PARAMS,
        name="gram",
    )(keep, sent)

    field = state
    owns = []
    recvs = []
    bits = [1 << k for k in range(groups.bit_length() - 1)]
    rounds = [[0] + bits[0:1], bits[1:3], bits[3:5], bits[5:]]
    for step in range(STEPS):
        zlo = lax.ppermute(zup, "solver", rise)
        zhi = lax.ppermute(zdn, "solver", fall)
        yin = lax.ppermute(yout, "ana", swap)
        for bit in rounds[step]:
            if bit:
                gram = gram + lax.ppermute(gram, "solver", [(i, i ^ bit) for i in range(groups)])
            else:
                gram = gram + lax.ppermute(theirs, "ana", swap)
        zlo, gram = lax.optimization_barrier((zlo, gram))
        if step:
            recvs.append(yin[RIM:])
        last = step == STEPS - 1
        outs = [shape((HALF, CP))]
        if last:
            outs = outs + [shape((HALF, CP)), shape((EL, C))]
        else:
            outs = [
                shape((EL, C)),
                shape((EL, 768), BF16),
                shape((EL, 768), BF16),
                shape((RIM, 128)),
                shape((RIM, 128)),
                shape((RIM + HALF, CP)),
            ] + outs
        res = pl.pallas_call(
            functools.partial(step_kernel, last),
            in_specs=[SMEM, SMEM] + [VMEM] * 11,
            out_shape=tuple(outs),
            compiler_params=PARAMS,
            name="step",
        )(order, ana, field, chi, clo, gd, snd, sel, w, m, zlo, zhi, yin)
        if last:
            own, rows_out = res[0], res[1]
        else:
            field, chi, clo, zdn, zup, yout, own = res
        owns.append(own)
    recvs.append(lax.ppermute(rows_out, "ana", swap))
    fields = jnp.stack([jnp.stack(owns, axis=1), jnp.stack(recvs, axis=1)]).reshape(SNAPS, CP)

    up, inv = pl.pallas_call(
        functools.partial(factor_kernel, scale),
        in_specs=[VMEM],
        out_shape=(shape((SNAPS, SNAPS)), shape((SNAPS, SNAPS))),
        compiler_params=PARAMS,
        name="factor",
    )(gram)

    rows, turned = pl.pallas_call(
        rows_kernel,
        in_specs=[VMEM, VMEM, VMEM],
        out_shape=(shape((groups, STEPS, SNAPS)), shape((C, 2 * SNAPS), BF16)),
        compiler_params=PARAMS,
        name="rows",
    )(fields, keep, other)
    gathered = lax.all_to_all(rows, "solver", 0, 0, tiled=True)

    wide, wf, fac = pl.pallas_call(
        functools.partial(border_kernel, scale),
        in_specs=[VMEM, VMEM, VMEM],
        out_shape=(shape((SNAPS, 2 * SNAPS), BF16), shape((2 * SNAPS, 2 * SNAPS), BF16), shape((1, SNAPS, SNAPS))),
        compiler_params=PARAMS,
        name="border",
    )(gathered, up, inv)

    coef = pl.pallas_call(
        final_kernel,
        grid=(HALF // 2,),
        in_specs=[SMEM] + [VMEM] * 5,
        out_specs=pl.BlockSpec((2, 2, C, SNAPS), lambda i: (0, i, 0, 0)),
        out_shape=shape((2, HALF, C, SNAPS)),
        compiler_params=PARAMS,
        name="final",
    )(ana, wide, wf, turned, keep, other)
    return coef.reshape(EL, C, SNAPS), fac


def solution(mesh):
    return jax.shard_map(
        body,
        mesh=mesh,
        in_specs=(
            P(("solver", "ana"), None),
            P(None, ("solver", "ana"), None),
            P(None, None, ("solver", "ana")),
            P(),
            P(),
            P(None, ("solver", "ana")),
            P(("solver", "ana")),
        ),
        out_specs=(P(("solver", "ana"), None, None), P("ana", None, None)),
        check_vma=False,
    )
```

time: 479 us -> 121 us (0.25); the launches traced: 470 us -> 119 us
  waiting for transfers between devices: 164 us -> 25.4 us
  local copies, waits for them, and re-layouts: 125 us -> 4.66 us
  other arithmetic: 61.5 us -> 0.11 us
  Pallas kernels: 0 us -> 40 us
  matrix products: 31.4 us -> 0 us
  blocking collectives: 15.7 us -> 0 us
  between operations: 15.6 us -> 0.94 us
  starting transfers between devices: 57.1 us -> 48.1 us
    psum x1 -> x0, waiting for transfers between devices: 163 us -> none  [body(): total = lax.psum(gram, 'solver')]
    concatenate x10 -> x0, local copies, waits for them, and re-layouts: 60.2 us -> none  [the longest x6 59.8 us: body(): jnp.concatenate([old_rows.astype(jnp.float32), owned], axis=0)]
    gather x85 -> x0, local copies, waits for them, and re-layouts: 44 us -> none  [the longest x40 15.2 us: body(): jnp.take(shaped, table[face], axis=2).reshape(elements, FC)]
    pallas_call x0 -> x12, Pallas kernels: none -> 40 us  [the longest x1 14.2 us: body(): pl.pallas_call(functools.partial(factor_kernel, scale), in_specs=[VMEM],...]
    another operation x20 -> x3, other arithmetic: 25.7 us -> 0.03 us  [body(): jnp.stack([jnp.stack(owns, axis=1), jnp.stack(recvs, axis=1)])]
    ppermute x16 -> x22, waiting for transfers between devices: 0.68 us -> 24.8 us  [the longest x7 15.7 us: body(): lax.ppermute(gram, 'solver', [(i, i ^ bit) for i in range(groups)])]
    dot_general x13 -> x0, matrix products: 23.6 us -> none  [the longest x1 13.1 us: body(): gram = jnp.dot(block, block.T, precision=highest) / region_rows]
    ppermute x16 -> x22, starting transfers between devices: 52.8 us -> 33.8 us  [the longest x4 24.6 us: body(): zhi = lax.ppermute(zdn, 'solver', fall)]
  transfers between devices with their start and end apart: 18 -> 23, of which waited for: 2 -> 11; matrix products, arithmetic and copies ran while one was open for 23% -> 1% of each run, Pallas kernels for 0% -> 19%
where the time goes in v1:
time: 121 us; the launch traced here: 119 us
  starting transfers between devices  48.1 us (40%)
  Pallas kernels  40 us (33%)
  waiting for transfers between devices  25.4 us (21%)
  local copies, waits for them, and re-layouts  4.66 us (4%)
    ppermute x4, starting transfers between devices, body(): zhi = lax.ppermute(zdn, 'solver', fall)  24.6 us
    ppermute x7, waiting for transfers between devices, body(): lax.ppermute(gram, 'solver', [(i, i ^ bit) for i in range(groups)])  15.7 us
    all_to_all x1, starting transfers between devices, body(): gathered = lax.all_to_all(rows, 'solver', 0, 0, tiled=True)  14.3 us
    pallas_call x1, Pallas kernels, body(): pl.pallas_call(functools.partial(factor_kernel, scale), in_specs=[VMEM],...  14.2 us
    pallas_call x4, Pallas kernels, body(): pl.pallas_call(functools.partial(step_kernel, last), in_specs=[SMEM, SMEM...  8.38 us
    ppermute x7, starting transfers between devices, body(): lax.ppermute(gram, 'solver', [(i, i ^ bit) for i in range(groups)])  7.58 us
    pallas_call x1, Pallas kernels, body(): pl.pallas_call(final_kernel, grid=(HALF // 2,), in_specs=[SMEM] + [VMEM]...  5.92 us
    pallas_call x1, Pallas kernels, body(): pl.pallas_call(pick_kernel, in_specs=[SMEM, SMEM, ANY], out_shape=(shape(...  5.41 us
  transfers between devices with their start and end apart: 23, of which 11 were waited for; matrix products, arithmetic and copies ran while one was open for 1% of the time, Pallas kernels for 19%

profile of v1, /device:TPU:2, one launch (start us, length us, event | category | flops | bytes accessed | tf_op | source)
XLA Modules:
  0.0 119.3 jit_solution(16548442144723720685)
XLA Ops:
  3.4 1.7 %copy-done = bf16[124,32,320]{0,2,1:T(8,128)(2,1)S(1)} copy-done((bf16[124,32,320]{0,2,1:T(8,128)(2,1)S(1)}, bf16[124,32,320]{0,2,1:T(8,128)(2,1)}, u32[]{:S(2)}) %copy-start) | copy-done | bytes 2539544
  5.1 5.4 %pick.1 = (bf16[16,320,124]{2,1,0:T(8,128)(2,1)S(1)}, bf16[16,320,124]{2,1,0:T(8,128)(2,1)}) custom-call(s32[1,32]{1,0:T(1,128)S(1)} %get-tuple-element.55.order_ref, s32[1]{0:T(128)} %bitcast.ana_ref, bf16[32,320,124]{2,1,0:T(8,128)(2,1)S(1)} %bitcast.23), custom_call_target="tpu_custom_call" | custom-call | tf_op jit(solution)/shard_map/pick/pallas_call | solution.py:419
  10.5 2.3 %gram.1 = (f32[128,128]{1,0:T(8,128)S(1)}, f32[128,128]{1,0:T(8,128)S(1)}) custom-call(bf16[16,320,124]{2,1,0:T(8,128)(2,1)S(1)} %get-tuple-element.64.keep_ref, bf16[16,320,124]{2,1,0:T(8,128)(2,1)} %get-tuple-element.65.sent_ref), custom_call_target="tpu_custom_call" | custom-call | tf_op jit(solution)/shard_map/gram/pallas_call | solution.py:437
  14.2 2.4 %collective-permute-start.2 = (f32[128,128]{1,0:T(8,128)S(1)}, f32[128,128]{1,0:T(8,128)S(1)}, u32[]{:S(2)}, u32[]{:S(2)}) collective-permute-start(f32[128,128]{1,0:T(8,128)S(1)} %add.28), channel_id=1, source_target_pairs={{0,2},{2,0},{4,6},{6,4},{8,10},{10,8},{12,14},{14,12},{16,18},{18,... | collective-permute-start | bytes 196616 | tf_op jit(solution)/shard_map/ppermute | solution.py:456
  17.0 2.0 %collective-permute-done.2 = f32[128,128]{1,0:T(8,128)S(1)} collective-permute-done((f32[128,128]{1,0:T(8,128)S(1)}, f32[128,128]{1,0:T(8,128)S(1)}, u32[]{:S(2)}, u32[]{:S(2)}) %collective-permute-start.2) | collective-permute-done | bytes 65568 | tf_op jit(solution)/shard_map/ppermute | solution.py:456
  20.8 5.1 %collective-permute-done.6 = f32[128,128]{1,0:T(8,128)S(1)} collective-permute-done((f32[128,128]{1,0:T(8,128)S(1)}, f32[128,128]{1,0:T(8,128)S(1)}, u32[]{:S(2)}, u32[]{:S(2)}) %collective-permute-start.6) | collective-permute-done | bytes 65568 | tf_op jit(solution)/shard_map/ppermute | solution.py:456
  26.1 7.5 %collective-permute-start.3 = (f32[8,128]{1,0:T(8,128)S(1)}, f32[8,128]{1,0:T(8,128)S(1)}, u32[]{:S(2)}, u32[]{:S(2)}) collective-permute-start(f32[8,128]{1,0:T(8,128)S(1)} %get-tuple-element.69), channel_id=1, source_target_pairs={{2,0},{4,2},{6,4},{8,6},{10,8},{12,10},{14,12},{16,14},{18,16},{20... | collective-permute-start | bytes 12296 | tf_op jit(solution)/shard_map/ppermute | solution.py:452
  35.0 2.0 %step.4 = (f32[32,320]{1,0:T(8,128)S(1)}, bf16[32,768]{1,0:T(8,128)(2,1)S(1)}, bf16[32,768]{1,0:T(8,128)(2,1)S(1)}, f32[8,128]{1,0:T(8,128)S(1)}, f32[8,128]{1,0...) custom-call(s32[1,32]{1,0:T(1,128)S(1)} %get-tuple-element.55.order_ref, s32[1]{0:T(128)} %bitcast.ana_ref, ...), custom_call_target="tpu_custom_call" | custom-call | tf_op jit(solution)/shard_map/step/pallas_call | solution.py:475
  37.4 4.0 %collective-permute-done.5.zlo_ref = f32[8,128]{1,0:T(8,128)S(1)} collective-permute-done((f32[8,128]{1,0:T(8,128)S(1)}, f32[8,128]{1,0:T(8,128)S(1)}, u32[]{:S(2)}, u32[]{:S(2)}) %collective-permute-start.5) | collective-permute-done | bytes 4128 | tf_op jit(solution)/shard_map/ppermute | solution.py:451
  41.4 7.7 %collective-permute-start.8 = (f32[8,128]{1,0:T(8,128)S(1)}, f32[8,128]{1,0:T(8,128)S(1)}, u32[]{:S(2)}, u32[]{:S(2)}) collective-permute-start(f32[8,128]{1,0:T(8,128)S(1)} %get-tuple-element.78), channel_id=1, source_target_pairs={{2,0},{4,2},{6,4},{8,6},{10,8},{12,10},{14,12},{16,14},{18,16},{20... | collective-permute-start | bytes 12296 | tf_op jit(solution)/shard_map/ppermute | solution.py:452
  49.1 1.3 %collective-permute-done.8.zhi_ref = f32[8,128]{1,0:T(8,128)S(1)} collective-permute-done((f32[8,128]{1,0:T(8,128)S(1)}, f32[8,128]{1,0:T(8,128)S(1)}, u32[]{:S(2)}, u32[]{:S(2)}) %collective-permute-start.8) | collective-permute-done | bytes 4128 | tf_op jit(solution)/shard_map/ppermute | solution.py:452
  50.4 2.0 %step.5 = (f32[32,320]{1,0:T(8,128)S(1)}, bf16[32,768]{1,0:T(8,128)(2,1)S(1)}, bf16[32,768]{1,0:T(8,128)(2,1)S(1)}, f32[8,128]{1,0:T(8,128)S(1)}, f32[8,128]{1,0...) custom-call(s32[1,32]{1,0:T(1,128)S(1)} %get-tuple-element.55.order_ref, s32[1]{0:T(128)} %bitcast.ana_ref, ...), custom_call_target="tpu_custom_call" | custom-call | tf_op jit(solution)/shard_map/step/pallas_call | solution.py:475
  52.6 2.4 %collective-permute-start.13 = (f32[8,128]{1,0:T(8,128)S(1)}, f32[8,128]{1,0:T(8,128)S(1)}, u32[]{:S(2)}, u32[]{:S(2)}) collective-permute-start(f32[8,128]{1,0:T(8,128)S(1)} %get-tuple-element.87), channel_id=1, source_target_pairs={{2,0},{4,2},{6,4},{8,6},{10,8},{12,10},{14,12},{16,14},{18,16},{20... | collective-permute-start | bytes 12296 | tf_op jit(solution)/shard_map/ppermute | solution.py:452
  55.1 4.5 %collective-permute-done.12 = f32[128,128]{1,0:T(8,128)S(1)} collective-permute-done((f32[128,128]{1,0:T(8,128)S(1)}, f32[128,128]{1,0:T(8,128)S(1)}, u32[]{:S(2)}, u32[]{:S(2)}) %collective-permute-start.12) | collective-permute-done | bytes 65568 | tf_op jit(solution)/shard_map/ppermute | solution.py:456
  59.6 2.0 %step.6 = (f32[32,320]{1,0:T(8,128)S(1)}, bf16[32,768]{1,0:T(8,128)(2,1)S(1)}, bf16[32,768]{1,0:T(8,128)(2,1)S(1)}, f32[8,128]{1,0:T(8,128)S(1)}, f32[8,128]{1,0...) custom-call(s32[1,32]{1,0:T(1,128)S(1)} %get-tuple-element.55.order_ref, s32[1]{0:T(128)} %bitcast.ana_ref, ...), custom_call_target="tpu_custom_call" | custom-call | tf_op jit(solution)/shard_map/step/pallas_call | solution.py:475
  62.5 7.0 %collective-permute-start.18 = (f32[8,128]{1,0:T(8,128)S(1)}, f32[8,128]{1,0:T(8,128)S(1)}, u32[]{:S(2)}, u32[]{:S(2)}) collective-permute-start(f32[8,128]{1,0:T(8,128)S(1)} %get-tuple-element.96), channel_id=1, source_target_pairs={{2,0},{4,2},{6,4},{8,6},{10,8},{12,10},{14,12},{16,14},{18,16},{20... | collective-permute-start | bytes 12296 | tf_op jit(solution)/shard_map/ppermute | solution.py:452
  69.5 4.1 %collective-permute-start.17 = (f32[128,128]{1,0:T(8,128)S(1)}, f32[128,128]{1,0:T(8,128)S(1)}, u32[]{:S(2)}, u32[]{:S(2)}) collective-permute-start(f32[128,128]{1,0:T(8,128)S(1)} %add.34), channel_id=1, source_target_pairs={{0,128},{2,130},{4,132},{6,134},{8,136},{10,138},{12,140},{14,142}... | collective-permute-start | bytes 196616 | tf_op jit(solution)/shard_map/ppermute | solution.py:456
  73.6 4.1 %collective-permute-done.17 = f32[128,128]{1,0:T(8,128)S(1)} collective-permute-done((f32[128,128]{1,0:T(8,128)S(1)}, f32[128,128]{1,0:T(8,128)S(1)}, u32[]{:S(2)}, u32[]{:S(2)}) %collective-permute-start.17) | collective-permute-done | bytes 65568 | tf_op jit(solution)/shard_map/ppermute | solution.py:456
  77.8 2.3 %step.7 = (f32[16,384]{1,0:T(8,128)S(1)}, f32[16,384]{1,0:T(8,128)S(1)}, f32[32,320]{1,0:T(8,128)}) custom-call(s32[1,32]{1,0:T(1,128)S(1)} %get-tuple-element.55.order_ref, s32[1]{0:T(128)} %bitcast.ana_ref, f32[32,320]{1,0:T(8,128)S(1)} %get-tuple-element.90.field_ref, bf16[32,768]{1,0:T(8,128)(2,1)S(1)} %get-tuple-element.91.chi_ref, ...), custom_call_target="tpu_custom_call" | custom-call | tf_op jit(solution)/shard_map/step/pallas_call | solution.py:475
  81.5 1.3 %rows.1 = (f32[128,4,128]{2,1,0:T(4,128)}, bf16[320,256]{1,0:T(8,128)(2,1)S(1)}) custom-call(f32[128,384]{1,0:T(8,128)S(1)} %reshape.26.fields_ref, bf16[16,320,124]{2,1,0:T(8,128)(2,1)S(1)} %get-tuple-element.64.keep_ref, bf16[16,320,124]{2,1,0:T(8,128)(2,1)S(1)} %collective-permute-done.21.other_ref), custom_call_target="tpu_custom_call" | custom-call | tf_op jit(solution)/shard_map/rows/pallas_call | solution.py:498
  82.8 14.3 %all-to-all-start = ((f32[128,4,128]{2,1,0:T(4,128)}), f32[128,4,128]{2,1,0:T(4,128)S(1)}, u32[]{:S(2)}, u32[]{:S(2)}) async-start(f32[128,4,128]{2,1,0:T(4,128)} %get-tuple-element.100), calls=%async_computation | async-start | bytes 524288 | tf_op jit(solution)/shard_map/all_to_all | solution.py:505
  97.0 14.2 %factor.1 = (f32[128,128]{1,0:T(8,128)S(1)}, f32[128,128]{1,0:T(8,128)S(1)}) custom-call(f32[128,128]{1,0:T(8,128)S(1)} %add.35.gram_ref), custom_call_target="tpu_custom_call" | custom-call | tf_op jit(solution)/shard_map/factor/pallas_call | solution.py:490
  111.9 1.4 %border.1 = (bf16[128,256]{1,0:T(8,128)(2,1)S(1)}, bf16[256,256]{1,0:T(8,128)(2,1)S(1)}, f32[1,128,128]{2,1,0:T(8,128)}) custom-call(f32[128,4,128]{2,1,0:T(4,128)S(1)} %all-to-all-done.gathered_ref, f32[128,128]{1,0:T(8,128)S(1)} %get-tuple-element.102.up_ref, f32[128,128]{1,0:T(8,128)S(1)} %get-tuple-element.103.inv_ref), custom_call_target="tpu_custom_call" | custom-call | tf_op jit(solution)/shard_map/border/pallas_call | solution.py:507
  113.3 5.9 %final.1 = f32[2,16,320,128]{3,2,1,0:T(8,128)} custom-call(s32[1]{0:T(128)} %bitcast.ana_ref, bf16[128,256]{1,0:T(8,128)(2,1)S(1)} %get-tuple-element.104.w_ref, bf16[256,256]{1,0:T(8,128)(2,1)S(1)} %get-tuple-element.105.wf_ref, bf16[320,256]{1,0:T(8,128)(2,1)S(1)} %get-tuple-element.106.turned_ref, bf16[16,320,124]{2,1,0:T(8,128)(2,1)S(1)} %get-tuple-element.64.keep_ref, ...), custom_call_target="tpu_custom_call" | custom-call | tf_op jit(solution)/shard_map/final/pallas_call | solution.py:515
  (67 shorter events, 11.3 us)
Async XLA Ops:
  10.5 23.2 %copy-start.7 = (f32[64,64,32]{1,2,0:T(8,128)S(1)}, f32[64,64,32]{1,2,0:T(8,128)}, u32[]{:S(2)}) copy-start(f32[64,64,32]{1,2,0:T(8,128)} %param.9) | copy-start | bytes 1572868
  12.8 1.3 %collective-permute-start.1 = (f32[128,128]{1,0:T(8,128)S(1)}, f32[128,128]{1,0:T(8,128)S(1)}, u32[]{:S(2)}, u32[]{:S(2)}) collective-permute-start(f32[128,128]{1,0:T(8,128)S(1)} %get-tuple-element.67), channel_id=1, source_target_pairs={{0,1},{1,0},{2,3},{3,2},{4,5},{5,4},{6,7},{7,6},{8,9},{9,8},{10,11... | collective-permute-start | bytes 196616 | tf_op jit(solution)/shard_map/ppermute | solution.py:458
  14.2 4.8 %collective-permute-start.2 = (f32[128,128]{1,0:T(8,128)S(1)}, f32[128,128]{1,0:T(8,128)S(1)}, u32[]{:S(2)}, u32[]{:S(2)}) collective-permute-start(f32[128,128]{1,0:T(8,128)S(1)} %add.28), channel_id=1, source_target_pairs={{0,2},{2,0},{4,6},{6,4},{8,10},{10,8},{12,14},{14,12},{16,18},{18,... | collective-permute-start | bytes 196616 | tf_op jit(solution)/shard_map/ppermute | solution.py:456
  16.5 64.9 %collective-permute-start.21 = (bf16[16,320,124]{2,1,0:T(8,128)(2,1)}, bf16[16,320,124]{2,1,0:T(8,128)(2,1)S(1)}, u32[]{:S(2)}, u32[]{:S(2)}) collective-permute-start(bf16[16,320,124]{2,1,0:T(8,128)(2,1)} %get-tuple-element.65.sent_ref), channel_id=1, source_target_pairs={{0,1},{1,0},{2,3},{3,2},{4,5},{5,4},{6,7},{7,6},{8,9},{9,8},{10,11... | collective-permute-start | bytes 3809288 | tf_op jit(solution)/shard_map/ppermute | solution.py:427
  16.6 3.6 %collective-permute-start = (f32[8,128]{1,0:T(8,128)S(1)}, f32[8,128]{1,0:T(8,128)S(1)}, u32[]{:S(2)}, u32[]{:S(2)}) collective-permute-start(f32[8,128]{1,0:T(8,128)S(1)} %get-tuple-element.63), channel_id=1, source_target_pairs={{0,2},{2,4},{4,6},{6,8},{8,10},{10,12},{12,14},{14,16},{16,18},{18... | collective-permute-start | bytes 12296 | tf_op jit(solution)/shard_map/ppermute | solution.py:451
  20.2 5.8 %collective-permute-start.6 = (f32[128,128]{1,0:T(8,128)S(1)}, f32[128,128]{1,0:T(8,128)S(1)}, u32[]{:S(2)}, u32[]{:S(2)}) collective-permute-start(f32[128,128]{1,0:T(8,128)S(1)} %add.29), channel_id=1, source_target_pairs={{0,4},{2,6},{4,0},{6,2},{8,12},{10,14},{12,8},{14,10},{16,20},{18,... | collective-permute-start | bytes 196616 | tf_op jit(solution)/shard_map/ppermute | solution.py:456
  25.9 11.4 %collective-permute-start.7 = (f32[128,128]{1,0:T(8,128)S(1)}, f32[128,128]{1,0:T(8,128)S(1)}, u32[]{:S(2)}, u32[]{:S(2)}) collective-permute-start(f32[128,128]{1,0:T(8,128)S(1)} %add.30), channel_id=1, source_target_pairs={{0,8},{2,10},{4,12},{6,14},{8,0},{10,2},{12,4},{14,6},{16,24},{18,... | collective-permute-start | bytes 196616 | tf_op jit(solution)/shard_map/ppermute | solution.py:456
  26.1 8.9 %collective-permute-start.3 = (f32[8,128]{1,0:T(8,128)S(1)}, f32[8,128]{1,0:T(8,128)S(1)}, u32[]{:S(2)}, u32[]{:S(2)}) collective-permute-start(f32[8,128]{1,0:T(8,128)S(1)} %get-tuple-element.69), channel_id=1, source_target_pairs={{2,0},{4,2},{6,4},{8,6},{10,8},{12,10},{14,12},{16,14},{18,16},{20... | collective-permute-start | bytes 12296 | tf_op jit(solution)/shard_map/ppermute | solution.py:452
  33.7 1.3 %collective-permute-start.4 = (f32[8,128]{1,0:T(8,128)S(1)}, f32[8,128]{1,0:T(8,128)S(1)}, u32[]{:S(2)}, u32[]{:S(2)}) collective-permute-start(f32[8,128]{1,0:T(8,128)S(1)} %get-tuple-element.70), channel_id=1, source_target_pairs={{0,1},{1,0},{2,3},{3,2},{4,5},{5,4},{6,7},{7,6},{8,9},{9,8},{10,11... | collective-permute-start | bytes 12296 | tf_op jit(solution)/shard_map/ppermute | solution.py:453
  37.1 4.3 %collective-permute-start.5 = (f32[8,128]{1,0:T(8,128)S(1)}, f32[8,128]{1,0:T(8,128)S(1)}, u32[]{:S(2)}, u32[]{:S(2)}) collective-permute-start(f32[8,128]{1,0:T(8,128)S(1)} %get-tuple-element.75), channel_id=1, source_target_pairs={{0,2},{2,4},{4,6},{6,8},{8,10},{10,12},{12,14},{14,16},{16,18},{18... | collective-permute-start | bytes 12296 | tf_op jit(solution)/shard_map/ppermute | solution.py:451
  41.4 13.5 %collective-permute-start.11 = (f32[128,128]{1,0:T(8,128)S(1)}, f32[128,128]{1,0:T(8,128)S(1)}, u32[]{:S(2)}, u32[]{:S(2)}) collective-permute-start(f32[128,128]{1,0:T(8,128)S(1)} %add.31), channel_id=1, source_target_pairs={{0,16},{2,18},{4,20},{6,22},{8,24},{10,26},{12,28},{14,30},{16,0},... | collective-permute-start | bytes 196616 | tf_op jit(solution)/shard_map/ppermute | solution.py:456
  41.4 9.0 %collective-permute-start.9 = (f32[24,384]{1,0:T(8,128)S(1)}, f32[24,384]{1,0:T(8,128)S(1)}, u32[]{:S(2)}, u32[]{:S(2)}) collective-permute-start(f32[24,384]{1,0:T(8,128)S(1)} %get-tuple-element.79), channel_id=1, source_target_pairs={{0,1},{1,0},{2,3},{3,2},{4,5},{5,4},{6,7},{7,6},{8,9},{9,8},{10,11... | collective-permute-start | bytes 110600 | tf_op jit(solution)/shard_map/ppermute | solution.py:453
  41.4 9.0 %collective-permute-start.8 = (f32[8,128]{1,0:T(8,128)S(1)}, f32[8,128]{1,0:T(8,128)S(1)}, u32[]{:S(2)}, u32[]{:S(2)}) collective-permute-start(f32[8,128]{1,0:T(8,128)S(1)} %get-tuple-element.78), channel_id=1, source_target_pairs={{2,0},{4,2},{6,4},{8,6},{10,8},{12,10},{14,12},{16,14},{18,16},{20... | collective-permute-start | bytes 12296 | tf_op jit(solution)/shard_map/ppermute | solution.py:452
  52.5 7.1 %collective-permute-start.10 = (f32[8,128]{1,0:T(8,128)S(1)}, f32[8,128]{1,0:T(8,128)S(1)}, u32[]{:S(2)}, u32[]{:S(2)}) collective-permute-start(f32[8,128]{1,0:T(8,128)S(1)} %get-tuple-element.84), channel_id=1, source_target_pairs={{0,2},{2,4},{4,6},{6,8},{8,10},{10,12},{12,14},{14,16},{16,18},{18... | collective-permute-start | bytes 12296 | tf_op jit(solution)/shard_map/ppermute | solution.py:451
  52.6 7.0 %collective-permute-start.13 = (f32[8,128]{1,0:T(8,128)S(1)}, f32[8,128]{1,0:T(8,128)S(1)}, u32[]{:S(2)}, u32[]{:S(2)}) collective-permute-start(f32[8,128]{1,0:T(8,128)S(1)} %get-tuple-element.87), channel_id=1, source_target_pairs={{2,0},{4,2},{6,4},{8,6},{10,8},{12,10},{14,12},{16,14},{18,16},{20... | collective-permute-start | bytes 12296 | tf_op jit(solution)/shard_map/ppermute | solution.py:452
  54.9 4.6 %collective-permute-start.14 = (f32[24,384]{1,0:T(8,128)S(1)}, f32[24,384]{1,0:T(8,128)S(1)}, u32[]{:S(2)}, u32[]{:S(2)}) collective-permute-start(f32[24,384]{1,0:T(8,128)S(1)} %get-tuple-element.88), channel_id=1, source_target_pairs={{0,1},{1,0},{2,3},{3,2},{4,5},{5,4},{6,7},{7,6},{8,9},{9,8},{10,11... | collective-permute-start | bytes 110600 | tf_op jit(solution)/shard_map/ppermute | solution.py:453
  54.9 4.6 %collective-permute-start.12 = (f32[128,128]{1,0:T(8,128)S(1)}, f32[128,128]{1,0:T(8,128)S(1)}, u32[]{:S(2)}, u32[]{:S(2)}) collective-permute-start(f32[128,128]{1,0:T(8,128)S(1)} %add.32), channel_id=1, source_target_pairs={{0,32},{2,34},{4,36},{6,38},{8,40},{10,42},{12,44},{14,46},{16,48}... | collective-permute-start | bytes 196616 | tf_op jit(solution)/shard_map/ppermute | solution.py:456
  61.6 12.0 %collective-permute-start.19 = (f32[24,384]{1,0:T(8,128)S(1)}, f32[24,384]{1,0:T(8,128)S(1)}, u32[]{:S(2)}, u32[]{:S(2)}) collective-permute-start(f32[24,384]{1,0:T(8,128)S(1)} %get-tuple-element.97), channel_id=1, source_target_pairs={{0,1},{1,0},{2,3},{3,2},{4,5},{5,4},{6,7},{7,6},{8,9},{9,8},{10,11... | collective-permute-start | bytes 110600 | tf_op jit(solution)/shard_map/ppermute | solution.py:453
  61.7 7.7 %collective-permute-start.16 = (f32[128,128]{1,0:T(8,128)S(1)}, f32[128,128]{1,0:T(8,128)S(1)}, u32[]{:S(2)}, u32[]{:S(2)}) collective-permute-start(f32[128,128]{1,0:T(8,128)S(1)} %add.33), channel_id=1, source_target_pairs={{0,64},{2,66},{4,68},{6,70},{8,72},{10,74},{12,76},{14,78},{16,80}... | collective-permute-start | bytes 196616 | tf_op jit(solution)/shard_map/ppermute | solution.py:456
  61.8 15.9 %collective-permute-start.15 = (f32[8,128]{1,0:T(8,128)S(1)}, f32[8,128]{1,0:T(8,128)S(1)}, u32[]{:S(2)}, u32[]{:S(2)}) collective-permute-start(f32[8,128]{1,0:T(8,128)S(1)} %get-tuple-element.93), channel_id=1, source_target_pairs={{0,2},{2,4},{4,6},{6,8},{8,10},{10,12},{12,14},{14,16},{16,18},{18... | collective-permute-start | bytes 12296 | tf_op jit(solution)/shard_map/ppermute | solution.py:451
  62.5 15.3 %collective-permute-start.18 = (f32[8,128]{1,0:T(8,128)S(1)}, f32[8,128]{1,0:T(8,128)S(1)}, u32[]{:S(2)}, u32[]{:S(2)}) collective-permute-start(f32[8,128]{1,0:T(8,128)S(1)} %get-tuple-element.96), channel_id=1, source_target_pairs={{2,0},{4,2},{6,4},{8,6},{10,8},{12,10},{14,12},{16,14},{18,16},{20... | collective-permute-start | bytes 12296 | tf_op jit(solution)/shard_map/ppermute | solution.py:452
  69.5 8.3 %collective-permute-start.17 = (f32[128,128]{1,0:T(8,128)S(1)}, f32[128,128]{1,0:T(8,128)S(1)}, u32[]{:S(2)}, u32[]{:S(2)}) collective-permute-start(f32[128,128]{1,0:T(8,128)S(1)} %add.34), channel_id=1, source_target_pairs={{0,128},{2,130},{4,132},{6,134},{8,136},{10,138},{12,140},{14,142}... | collective-permute-start | bytes 196616 | tf_op jit(solution)/shard_map/ppermute | solution.py:456
  80.1 1.2 %collective-permute-start.20 = (f32[16,384]{1,0:T(8,128)S(1)}, f32[16,384]{1,0:T(8,128)S(1)}, u32[]{:S(2)}, u32[]{:S(2)}) collective-permute-start(f32[16,384]{1,0:T(8,128)S(1)} %get-tuple-element.99), channel_id=1, source_target_pairs={{0,1},{1,0},{2,3},{3,2},{4,5},{5,4},{6,7},{7,6},{8,9},{9,8},{10,11... | collective-permute-start | bytes 73736 | tf_op jit(solution)/shard_map/ppermute | solution.py:487
  82.8 29.2 %all-to-all-start = ((f32[128,4,128]{2,1,0:T(4,128)}), f32[128,4,128]{2,1,0:T(4,128)S(1)}, u32[]{:S(2)}, u32[]{:S(2)}) async-start(f32[128,4,128]{2,1,0:T(4,128)} %get-tuple-element.100), calls=%async_computation | async-start | bytes 524288 | tf_op jit(solution)/shard_map/all_to_all | solution.py:505
  (7 other events, 48.2 us)

commit v2 on v1

--- a/solution.py
+++ b/solution.py
@@ -20,6 +20,8 @@
 HIST = 124
 SNAPS = 128
 STEPS = 4
+FOLD = 72
+FINAL = 2
 RIM = 8
 time_step = 0.2
 
@@ -43,16 +45,19 @@
     return out[:EL].astype(BF16), out[EL:].astype(BF16)
 
 
-def send_faces(snd, chi, clo):
+def send_faces(snd, chi, clo, parity):
     out = mm(snd, chi[:, 256:768]) + mm(snd, clo[:, 256:768])
+    below = out[0:8, 384:512]
+    above = out[8:16, 256:384]
+    even = parity == 0
     return (
-        out[0:8, 384:512],
-        out[8:16, 256:384],
+        jnp.where(even, above, below),
+        jnp.where(even, below, above),
         out[16:24, 128:256] + out[24:32, 0:128],
     )
 
 
-def setup_kernel(base_ref, nbr_any, own_any, state_any, gd_ref, snd_ref, order_ref, sel_ref, chi_ref, clo_ref, zdn_ref, zup_ref, y_ref, nbr_ref, own_ref, state_ref, sem):
+def setup_kernel(base_ref, place_ref, nbr_any, own_any, state_any, gd_ref, snd_ref, order_ref, sel_ref, chi_ref, clo_ref, zev_ref, zod_ref, y_ref, nbr_ref, own_ref, state_ref, sem):
     copies = [
         pltpu.make_async_copy(src, dst, sem.at[k])
         for k, (src, dst) in enumerate(((nbr_any, nbr_ref), (own_any, own_ref), (state_any, state_ref)))
@@ -114,7 +119,7 @@
     chi, clo = contacts(state_ref[...], sel)
     chi_ref[...] = chi
     clo_ref[...] = clo
-    zdn_ref[...], zup_ref[...], y_ref[...] = send_faces(snd, chi, clo)
+    zev_ref[...], zod_ref[...], y_ref[...] = send_faces(snd, chi, clo, place_ref[1])
 
 
 def prep_kernel(vol_ref, lift_ref, mass_ref, w_ref, m_ref):
@@ -132,7 +137,7 @@
     m_ref[:, NODES:128] = low
 
 
-def step_kernel(last, order_ref, ana_ref, field_ref, chi_ref, clo_ref, gd_ref, snd_ref, sel_ref, w_ref, m_ref, zlo_ref, zhi_ref, y_ref, *outs):
+def step_kernel(last, order_ref, place_ref, field_ref, chi_ref, clo_ref, gd_ref, snd_ref, sel_ref, w_ref, m_ref, even_ref, odd_ref, y_ref, *outs):
     rest = list(outs)
     new_ref = rest.pop() if last else rest.pop(0)
     field = field_ref[...]
@@ -141,7 +146,10 @@
     his = [fhi, pad]
     los = [flo, pad]
     y_in = y_ref[0:RIM, 0:128]
-    arrived = {2: y_in, 3: y_in, 4: zlo_ref[...], 5: zhi_ref[...]}
+    even = place_ref[1] == 0
+    by_even = even_ref[0:RIM]
+    by_odd = odd_ref[...]
+    arrived = {2: y_in, 3: y_in, 4: jnp.where(even, by_odd, by_even), 5: jnp.where(even, by_even, by_odd)}
     for face in range(6):
         lanes = slice(128 * face, 128 * face + 128)
         rows = jnp.concatenate([chi_ref[:, lanes], clo_ref[:, lanes]], axis=1)
@@ -175,19 +183,19 @@
         parts.append(jnp.concatenate([prod[HALF * var : HALF * var + HALF] for var in range(5)], axis=1))
     new = field + time_step * jnp.concatenate(parts, axis=0)
     new_ref[...] = new
-    ana = ana_ref[0]
+    ana = place_ref[0]
     if last:
         fown_ref, fsend_ref = rest
         first = 0
     else:
-        chi_out, clo_out, zdn_ref, zup_ref, fsend_ref, fown_ref = rest
+        chi_out, clo_out, zev_ref, zod_ref, fsend_ref, fown_ref = rest
         first = RIM
         chi, clo = contacts(new, sel_ref[...])
         chi_out[...] = chi
         clo_out[...] = clo
-        zdn, zup, y = send_faces(snd_ref[...], chi, clo)
-        zdn_ref[...] = zdn
-        zup_ref[...] = zup
+        zev, zod, y = send_faces(snd_ref[...], chi, clo, place_ref[1])
+        zev_ref[...] = zev
+        zod_ref[...] = zod
         fsend_ref[0:RIM, 0:128] = y
         fsend_ref[0:RIM, 128:CP] = jnp.zeros((RIM, CP - 128), F32)
     fsend_ref[first : first + HALF, C:CP] = jnp.zeros((HALF, CP - C), F32)
@@ -199,8 +207,8 @@
         fsend_ref[first + k : first + k + 1, 0:C] = new_ref[pl.ds(other, 1), :]
 
 
-def pick_kernel(order_ref, ana_ref, hist_ref, keep_ref, sent_ref, sem):
-    ana = ana_ref[0]
+def pick_kernel(order_ref, place_ref, hist_ref, keep_ref, sent_ref, sem):
+    ana = place_ref[0]
     copies = []
     for k in range(HALF):
         copies.append(pltpu.make_async_copy(hist_ref.at[order_ref[0, ana * HALF + k]], keep_ref.at[k], sem.at[k]))
@@ -213,54 +221,73 @@
         copy.wait()
 
 
-def gram_kernel(keep_ref, sent_ref, mine_ref, theirs_ref):
+def gram_kernel(keep_ref, sent_ref, mine_ref, theirs_ref, full_ref):
+    row = iota((64, SNAPS), 0)
+    col = iota((64, SNAPS), 1)
     for ref, out_ref in ((keep_ref, mine_ref), (sent_ref, theirs_ref)):
         total = None
         for k in range(0, HALF, 4):
             rows = ref[k : k + 4].reshape(4 * C, HIST)
             part = lax.dot_general(rows, rows, (((0,), (0,)), ((), ())), preferred_element_type=F32)
             total = part if total is None else total + part
-        out_ref[...] = jnp.zeros_like(out_ref)
-        out_ref[0:HIST, 0:HIST] = total
+        full_ref[...] = jnp.zeros_like(full_ref)
+        full_ref[0:HIST, 0:HIST] = total
+        last = pltpu.roll(full_ref[64:SNAPS], 64, 1)
+        out_ref[0:64] = jnp.where(col < row, last, full_ref[0:64])
+        diag = jnp.sum(jnp.where(col == row, last, 0.0), axis=0, keepdims=True)
+        out_ref[64:FOLD] = jnp.broadcast_to(diag, (FOLD - 64, SNAPS))
+
+
+def unfold(folded):
+    row = iota((64, SNAPS), 0)
+    col = iota((64, SNAPS), 1)
+    top = folded[0:64]
+    upper = jnp.where(col > row, top, 0.0)
+    lower = pltpu.roll(jnp.where(col < row, top, 0.0), 64, 1)
+    half = jnp.concatenate([upper, lower], axis=0)
+    last = pltpu.roll(jnp.broadcast_to(folded[64:65], (64, SNAPS)), 64, 1)
+    diag = jnp.concatenate([jnp.where(col == row, top, 0.0), jnp.where(col == row + 64, last, 0.0)], axis=0)
+    return half + half.T + diag
 
 
 def factor_kernel(scale, gram_ref, up_ref, inv_ref):
     tiles = SNAPS // 8
     row = iota((SNAPS, SNAPS), 0)
     col = iota((SNAPS, SNAPS), 1)
-    start = jnp.where((row < HIST) & (col < HIST), gram_ref[...] * scale, jnp.where(row == col, 1.0, 0.0))
+    start = jnp.where((row < HIST) & (col < HIST), unfold(gram_ref[...]) * scale, jnp.where(row == col, 1.0, 0.0))
     ident = jnp.where(row == col, 1.0, 0.0)
     a = [start[8 * t : 8 * t + 8] for t in range(tiles)]
     b = [ident[8 * t : 8 * t + 8] for t in range(tiles)]
     below = iota((8, SNAPS), 0)
+    full = (8, SNAPS)
     for j in range(0, HIST, 2):
         t = j // 8
         r = j % 8
-        a0 = a[t][r : r + 1, :]
-        a1 = a[t][r + 1 : r + 2, :]
-        b0 = b[t][r : r + 1, :]
-        b1 = b[t][r + 1 : r + 2, :]
-        p = a0[:, j : j + 1]
-        q = a0[:, j + 1 : j + 2]
-        s = a1[:, j + 1 : j + 2]
+        m0 = {k: jnp.broadcast_to(a[k][:, j : j + 1], full) for k in range(t, tiles)}
+        m1 = {k: jnp.broadcast_to(a[k][:, j + 1 : j + 2], full) for k in range(t, tiles)}
+        p = jnp.broadcast_to(m0[t][r : r + 1], full)
+        q = jnp.broadcast_to(m0[t][r + 1 : r + 2], full)
+        s = jnp.broadcast_to(m1[t][r + 1 : r + 2], full)
+        a0 = jnp.broadcast_to(a[t][r : r + 1], full)
+        a1 = jnp.broadcast_to(a[t][r + 1 : r + 2], full)
+        b0 = jnp.broadcast_to(b[t][r : r + 1], full)
+        b1 = jnp.broadcast_to(b[t][r + 1 : r + 2], full)
         inv = 1.0 / (p * s - q * q)
-        ip = jnp.broadcast_to(s * inv, (1, SNAPS))
-        iq = jnp.broadcast_to(q * inv, (1, SNAPS))
-        js = jnp.broadcast_to(p * inv, (1, SNAPS))
-        sa0 = jnp.broadcast_to(ip * a0 - iq * a1, (8, SNAPS))
-        sa1 = jnp.broadcast_to(js * a1 - iq * a0, (8, SNAPS))
-        sb0 = jnp.broadcast_to(ip * b0 - iq * b1, (8, SNAPS))
-        sb1 = jnp.broadcast_to(js * b1 - iq * b0, (8, SNAPS))
+        ip = s * inv
+        iq = q * inv
+        js = p * inv
+        sa0 = ip * a0 - iq * a1
+        sa1 = js * a1 - iq * a0
+        sb0 = ip * b0 - iq * b1
+        sb1 = js * b1 - iq * b0
         for k in range(t, tiles):
-            if k == t and r == 6:
-                continue
-            m0 = jnp.broadcast_to(a[k][:, j : j + 1], (8, SNAPS))
-            m1 = jnp.broadcast_to(a[k][:, j + 1 : j + 2], (8, SNAPS))
             if k == t:
-                m0 = jnp.where(below > r + 1, m0, 0.0)
-                m1 = jnp.where(below > r + 1, m1, 0.0)
-            a[k] = a[k] - m0 * sa0 - m1 * sa1
-            b[k] = b[k] - m0 * sb0 - m1 * sb1
+                if r == 6:
+                    continue
+                m0[k] = jnp.where(below > r + 1, m0[k], 0.0)
+                m1[k] = jnp.where(below > r + 1, m1[k], 0.0)
+            a[k] = a[k] - m0[k] * sa0 - m1[k] * sa1
+            b[k] = b[k] - m0[k] * sb0 - m1[k] * sb1
     up = jnp.concatenate(a, axis=0)
     low = jnp.concatenate(b, axis=0)
     odd = (iota((SNAPS, 1), 0) % 2) == 1
@@ -355,19 +382,31 @@
     fac_ref[0] = jnp.concatenate([upper[0:HIST], tri], axis=0)
 
 
-def final_kernel(ana_ref, w_ref, wf_ref, turned_ref, keep_ref, other_ref, out_ref):
-    i = pl.program_id(0)
-    ana = ana_ref[0]
+def final_kernel(place_ref, w_ref, wf_ref, turned_ref, keep_ref, other_ref, out_ref, buf_ref, sem):
+    ana = place_ref[0]
     main = w_ref[0:HIST, :]
-    ends = wf_ref[...].astype(F32)
+    ends = wf_ref[...]
     turned = turned_ref[...]
-    element = (iota((2 * SNAPS, 2 * SNAPS), 0) % SNAPS) // 4
-    for half, which, ref in ((0, ana, keep_ref), (1, 1 - ana, other_ref)):
-        for k in range(2):
-            at = 2 * i + k
-            tail = jnp.where(element == at + HALF * half, ends, 0.0).astype(BF16)
-            prod = mm(ref[at], main) + mm(turned, tail)
-            out_ref[which, k] = prod[:, 0:SNAPS] + prod[:, SNAPS : 2 * SNAPS]
+    element = (iota((1, 2 * SNAPS), 1) % SNAPS) // 4
+    copies = []
+    for at in range(0, HALF, FINAL):
+        for half, which, ref in ((0, ana, keep_ref), (1, 1 - ana, other_ref)):
+            own = [
+                turned * jnp.where(element == at + k + HALF * half, 1.0, 0.0).astype(BF16) for k in range(FINAL)
+            ]
+            rows = ref[at : at + FINAL].reshape(FINAL * C, HIST)
+            prod = mm(rows, main) + mm(jnp.concatenate(own, axis=0), ends)
+            prod = (prod[:, 0:SNAPS] + prod[:, SNAPS : 2 * SNAPS]).reshape(FINAL, C, SNAPS)
+            buf_ref[half, at : at + FINAL] = prod
+            copy = pltpu.make_async_copy(
+                buf_ref.at[half, pl.ds(at, FINAL)],
+                out_ref.at[which, pl.ds(at, FINAL)],
+                sem.at[len(copies)],
+            )
+            copy.start()
+            copies.append(copy)
+    for copy in copies:
+        copy.wait()
 
 
 def shape(dims, kind=F32):
@@ -376,25 +415,28 @@
 
 SMEM = pl.BlockSpec(memory_space=pltpu.SMEM)
 VMEM = pl.BlockSpec(memory_space=pltpu.VMEM)
-ANY = pl.BlockSpec(memory_space=pl.ANY)
+ANY = pl.BlockSpec(memory_space=pltpu.HBM)
 PARAMS = pltpu.CompilerParams(vmem_limit_bytes=40 << 20)
+
+
+def in_hbm(x):
+    return pltpu.with_memory_space_constraint(x, pltpu.HBM)
 
 
 def body(state, history, inv_mass, vol_op, lift_ops, neighbors, owner):
     groups = lax.axis_size("solver")
-    ana = lax.axis_index("ana").astype(I32)
+    place = jnp.stack([lax.axis_index("ana"), lax.axis_index("solver") % 2]).astype(I32)
     base = (lax.axis_index(("solver", "ana")) * EL).astype(I32).reshape(1)
-    ana = ana.reshape(1)
-    hist = jnp.transpose(history, (1, 2, 0))
+    hist = in_hbm(jnp.transpose(history, (1, 2, 0)))
     mass = jnp.transpose(inv_mass, (2, 0, 1)).reshape(EL * NODES, NODES)
     scale = 1.0 / (EL * C * groups)
-    rise = [(i, (i + 1) % groups) for i in range(groups)]
-    fall = [((i + 1) % groups, i) for i in range(groups)]
+    evens = [(i, i ^ 1) for i in range(groups)]
+    odds = [(i, (i + 1 if i % 2 else i - 1) % groups) for i in range(groups)]
     swap = [(0, 1), (1, 0)]
 
-    gd, snd, order, sel, chi, clo, zdn, zup, yout = pl.pallas_call(
+    gd, snd, order, sel, chi, clo, zev, zod, yout = pl.pallas_call(
         setup_kernel,
-        in_specs=[SMEM, ANY, ANY, ANY],
+        in_specs=[SMEM, SMEM, ANY, ANY, ANY],
         scratch_shapes=[
             pltpu.VMEM((6, EL), I32),
             pltpu.VMEM((1, EL), I32),
@@ -414,7 +456,7 @@
         ),
         compiler_params=PARAMS,
         name="setup",
-    )(base, neighbors, owner.reshape(1, EL), state)
+    )(base, place, in_hbm(neighbors), in_hbm(owner.reshape(1, EL)), in_hbm(state))
 
     keep, sent = pl.pallas_call(
         pick_kernel,
@@ -423,9 +465,7 @@
         scratch_shapes=[pltpu.SemaphoreType.DMA((2 * HALF,))],
         compiler_params=PARAMS,
         name="pick",
-    )(order, ana, hist)
-    other = lax.ppermute(sent, "ana", swap)
-
+    )(order, place, hist)
     w, m = pl.pallas_call(
         prep_kernel,
         in_specs=[VMEM, VMEM, VMEM],
@@ -437,26 +477,36 @@
     gram, theirs = pl.pallas_call(
         gram_kernel,
         in_specs=[VMEM, VMEM],
-        out_shape=(shape((SNAPS, SNAPS)), shape((SNAPS, SNAPS))),
+        out_shape=(shape((FOLD, SNAPS)), shape((FOLD, SNAPS))),
+        scratch_shapes=[pltpu.VMEM((SNAPS, SNAPS), F32)],
         compiler_params=PARAMS,
         name="gram",
     )(keep, sent)
-
     field = state
     owns = []
     recvs = []
     bits = [1 << k for k in range(groups.bit_length() - 1)]
-    rounds = [[0] + bits[0:1], bits[1:3], bits[3:5], bits[5:]]
+    stages = [[], bits[1:3], bits[3:5], bits[5:7], bits[0:1]]
+
+    def summed(gram, two):
+        total = gram
+        if not two:
+            return gram
+        for bit in two + ([two[0] | two[1]] if len(two) == 2 else []):
+            total = total + lax.ppermute(gram, "solver", [(i, i ^ bit) for i in range(groups)])
+        return total
+
     for step in range(STEPS):
-        zlo = lax.ppermute(zup, "solver", rise)
-        zhi = lax.ppermute(zdn, "solver", fall)
+        even = lax.ppermute(zev, "solver", evens)
+        gram = summed(gram, stages[step])
+        odd = lax.ppermute(zod, "solver", odds)
         yin = lax.ppermute(yout, "ana", swap)
-        for bit in rounds[step]:
-            if bit:
-                gram = gram + lax.ppermute(gram, "solver", [(i, i ^ bit) for i in range(groups)])
-            else:
-                gram = gram + lax.ppermute(theirs, "ana", swap)
-        zlo, gram = lax.optimization_barrier((zlo, gram))
+        if step == 0:
+            theirs, sent, even, odd, yin = lax.optimization_barrier((theirs, sent, even, odd, yin))
+            gram = gram + lax.ppermute(theirs, "ana", swap)
+            other = lax.ppermute(sent, "ana", swap)
+        else:
+            even, odd, yin, gram, other = lax.optimization_barrier((even, odd, yin, gram, other))
         if step:
             recvs.append(yin[RIM:])
         last = step == STEPS - 1
@@ -478,15 +528,17 @@
             out_shape=tuple(outs),
             compiler_params=PARAMS,
             name="step",
-        )(order, ana, field, chi, clo, gd, snd, sel, w, m, zlo, zhi, yin)
+        )(order, place, field, chi, clo, gd, snd, sel, w, m, even, odd, yin)
         if last:
             own, rows_out = res[0], res[1]
         else:
-            field, chi, clo, zdn, zup, yout, own = res
+            field, chi, clo, zev, zod, yout, own = res
+            gram, zev, zod, yout = lax.optimization_barrier((gram, zev, zod, yout))
         owns.append(own)
     recvs.append(lax.ppermute(rows_out, "ana", swap))
     fields = jnp.stack([jnp.stack(owns, axis=1), jnp.stack(recvs, axis=1)]).reshape(SNAPS, CP)
 
+    gram = summed(gram, stages[STEPS])
     up, inv = pl.pallas_call(
         functools.partial(factor_kernel, scale),
         in_specs=[VMEM],
@@ -514,13 +566,16 @@
 
     coef = pl.pallas_call(
         final_kernel,
-        grid=(HALF // 2,),
         in_specs=[SMEM] + [VMEM] * 5,
-        out_specs=pl.BlockSpec((2, 2, C, SNAPS), lambda i: (0, i, 0, 0)),
+        out_specs=ANY,
         out_shape=shape((2, HALF, C, SNAPS)),
+        scratch_shapes=[
+            pltpu.VMEM((2, HALF, C, SNAPS), F32),
+            pltpu.SemaphoreType.DMA((2 * HALF // FINAL,)),
+        ],
         compiler_params=PARAMS,
         name="final",
-    )(ana, wide, wf, turned, keep, other)
+    )(place, wide, wf, turned, keep, other)
     return coef.reshape(EL, C, SNAPS), fac
 
 

time: 121 us -> 106 us (0.88)
  waiting for transfers between devices: 25.4 us -> 16.1 us
  Pallas kernels: 40 us -> 31.1 us
  starting transfers between devices: 48.1 us -> 56.2 us
  local copies, waits for them, and re-layouts: 4.66 us -> 0.79 us
    ppermute x15 -> x18, starting transfers between devices: 33.6 us -> 42.4 us  [the longest x4 24 us: body(): even = lax.ppermute(zev, 'solver', evens)]
    ppermute x15 -> x18, waiting for transfers between devices: 22.3 us -> 13.9 us  [the longest x4 5.68 us: body(): odd = lax.ppermute(zod, 'solver', odds)]
    pallas_call x1, Pallas kernels: 14.2 us -> 9.37 us  [body(): pl.pallas_call(functools.partial(factor_kernel, scale), in_specs=[VMEM],...]
    unnamed x16 -> x8, local copies, waits for them, and re-layouts: 3.89 us -> 0.02 us
    pallas_call x1, Pallas kernels: 5.41 us -> 2.59 us  [body(): pl.pallas_call(pick_kernel, in_specs=[SMEM, SMEM, ANY], out_shape=(shape(...]
    pallas_call x3, Pallas kernels: 8.76 us -> 7.42 us  [the longest x1 4.56 us: body(): pl.pallas_call(final_kernel, in_specs=[SMEM] + [VMEM] * 5, out_specs=ANY,...]
    all_to_all x1, starting transfers between devices: 14.3 us -> 13 us  [body(): gathered = lax.all_to_all(rows, 'solver', 0, 0, tiled=True)]
    ppermute x1, waiting for transfers between devices: 1.24 us -> 0.01 us  [body(): gram = gram + lax.ppermute(theirs, 'ana', swap)]
  transfers between devices with their start and end apart: 23 -> 26, of which waited for: 11 -> 9; matrix products, arithmetic and copies ran while one was open for 1% -> 1% of each run, Pallas kernels for 19% -> 15%
where the time goes in v2:
time: 106 us; the launch traced here: 105 us
  starting transfers between devices  56.2 us (53%)
  Pallas kernels  31.1 us (29%)
  waiting for transfers between devices  16.1 us (15%)
  between operations  1.11 us (1%)
    ppermute x4, starting transfers between devices, body(): even = lax.ppermute(zev, 'solver', evens)  24 us
    ppermute x10, starting transfers between devices, summed(): lax.ppermute(gram, 'solver', [(i, i ^ bit) for i in range(groups)])  17.9 us
    all_to_all x1, starting transfers between devices, body(): gathered = lax.all_to_all(rows, 'solver', 0, 0, tiled=True)  13 us
    pallas_call x1, Pallas kernels, body(): pl.pallas_call(functools.partial(factor_kernel, scale), in_specs=[VMEM],...  9.37 us
    pallas_call x4, Pallas kernels, body(): pl.pallas_call(functools.partial(step_kernel, last), in_specs=[SMEM, SMEM...  8.4 us
    ppermute x4, waiting for transfers between devices, body(): odd = lax.ppermute(zod, 'solver', odds)  5.68 us
    ppermute x4, waiting for transfers between devices, body(): even = lax.ppermute(zev, 'solver', evens)  4.89 us
    pallas_call x1, Pallas kernels, body(): pl.pallas_call(final_kernel, in_specs=[SMEM] + [VMEM] * 5, out_specs=ANY,...  4.56 us
  transfers between devices with their start and end apart: 26, of which 9 were waited for; matrix products, arithmetic and copies ran while one was open for 1% of the time, Pallas kernels for 15%

profile of v2, /device:TPU:2, one launch (start us, length us, event | category | flops | bytes accessed | tf_op | source)
XLA Modules:
  0.0 105.5 jit_solution(18389921820185638879)
XLA Ops:
  0.7 1.9 %setup.1 = (bf16[6,32,48]{2,1,0:T(8,128)(2,1)S(1)}, bf16[32,32]{1,0:T(8,128)(2,1)S(1)}, s32[1,32]{1,0:T(1,128)S(1)}, bf16[320,768]{1,0:T(8,128)(2,1)S(1)}, bf16[...) custom-call(s32[1]{0:T(128)} %bitcast.2.base_ref, ...), custom_call_target="tpu_custom_call" | custom-call | tf_op jit(solution)/shard_map/setup/pallas_call | solution.py:437
  2.6 2.4 %collective-permute-start = (f32[8,128]{1,0:T(8,128)S(1)}, f32[8,128]{1,0:T(8,128)S(1)}, u32[]{:S(2)}, u32[]{:S(2)}) collective-permute-start(f32[8,128]{1,0:T(8,128)S(1)} %get-tuple-element.90), channel_id=1, source_target_pairs={{0,2},{2,0},{4,6},{6,4},{8,10},{10,8},{12,14},{14,12},{16,18},{18,... | collective-permute-start | bytes 12296 | tf_op jit(solution)/shard_map/ppermute | solution.py:500
  5.4 2.6 %pick.1 = (bf16[16,320,124]{2,1,0:T(8,128)(2,1)S(1)}, bf16[16,320,124]{2,1,0:T(8,128)(2,1)S(1)}) custom-call(s32[1,32]{1,0:T(1,128)S(1)} %get-tuple-element.79.order_ref, s32[2]{0:T(128)S(1)} %pad_add_fusion.place_ref, bf16[32,320,124]{2,1,0:T(8,128)(2,1)} %bitcast.29), custom_call_target="tpu_custom_call" | custom-call | tf_op jit(solution)/shard_map/pick/pallas_call | solution.py:461
  11.0 2.0 %step.4 = (f32[32,320]{1,0:T(8,128)S(1)}, bf16[32,768]{1,0:T(8,128)(2,1)S(1)}, bf16[32,768]{1,0:T(8,128)(2,1)S(1)}, f32[8,128]{1,0:T(8,128)S(1)}, f32[8,128]{1,0...) custom-call(s32[1,32]{1,0:T(1,128)S(1)} %get-tuple-element.79.order_ref, s32[2]{0:T(128)S(1)} %pad_add_fusion.place_ref, ...), custom_call_target="tpu_custom_call" | custom-call | tf_op jit(solution)/shard_map/step/pallas_call | solution.py:525
  13.1 3.5 %collective-permute-start.9 = (f32[72,128]{1,0:T(8,128)S(1)}, f32[72,128]{1,0:T(8,128)S(1)}, u32[]{:S(2)}, u32[]{:S(2)}) collective-permute-start(f32[72,128]{1,0:T(8,128)S(1)} %add.42), channel_id=1, source_target_pairs={{0,12},{2,14},{4,8},{6,10},{8,4},{10,6},{12,0},{14,2},{16,28},{18,... | collective-permute-start | bytes 110600 | tf_op jit(solution)/shard_map/ppermute | solution.py:496
  18.1 9.2 %collective-permute-start.4 = (f32[8,128]{1,0:T(8,128)S(1)}, f32[8,128]{1,0:T(8,128)S(1)}, u32[]{:S(2)}, u32[]{:S(2)}) collective-permute-start(f32[8,128]{1,0:T(8,128)S(1)} %get-tuple-element.105), channel_id=1, source_target_pairs={{0,2},{2,0},{4,6},{6,4},{8,10},{10,8},{12,14},{14,12},{16,18},{18,... | collective-permute-start | bytes 12296 | tf_op jit(solution)/shard_map/ppermute | solution.py:500
  27.4 1.8 %collective-permute-done.4.even_ref = f32[8,128]{1,0:T(8,128)S(1)} collective-permute-done((f32[8,128]{1,0:T(8,128)S(1)}, f32[8,128]{1,0:T(8,128)S(1)}, u32[]{:S(2)}, u32[]{:S(2)}) %collective-permute-start.4) | collective-permute-done | bytes 4128 | tf_op jit(solution)/shard_map/ppermute | solution.py:500
  29.3 1.6 %collective-permute-done.5.odd_ref = f32[8,128]{1,0:T(8,128)S(1)} collective-permute-done((f32[8,128]{1,0:T(8,128)S(1)}, f32[8,128]{1,0:T(8,128)S(1)}, u32[]{:S(2)}, u32[]{:S(2)}) %collective-permute-start.5) | collective-permute-done | bytes 4128 | tf_op jit(solution)/shard_map/ppermute | solution.py:502
  30.9 2.0 %step.5 = (f32[32,320]{1,0:T(8,128)S(1)}, bf16[32,768]{1,0:T(8,128)(2,1)S(1)}, bf16[32,768]{1,0:T(8,128)(2,1)S(1)}, f32[8,128]{1,0:T(8,128)S(1)}, f32[8,128]{1,0...) custom-call(s32[1,32]{1,0:T(1,128)S(1)} %get-tuple-element.79.order_ref, s32[2]{0:T(128)S(1)} %pad_add_fusion.place_ref, ...), custom_call_target="tpu_custom_call" | custom-call | tf_op jit(solution)/shard_map/step/pallas_call | solution.py:525
  33.2 4.9 %collective-permute-start.14 = (f32[72,128]{1,0:T(8,128)S(1)}, f32[72,128]{1,0:T(8,128)S(1)}, u32[]{:S(2)}, u32[]{:S(2)}) collective-permute-start(f32[72,128]{1,0:T(8,128)S(1)} %add_add_fusion.2), channel_id=1, source_target_pairs={{0,16},{2,18},{4,20},{6,22},{8,24},{10,26},{12,28},{14,30},{16,0},... | collective-permute-start | bytes 110600 | tf_op jit(solution)/shard_map/ppermute | solution.py:496
  38.0 7.1 %collective-permute-start.11 = (f32[8,128]{1,0:T(8,128)S(1)}, f32[8,128]{1,0:T(8,128)S(1)}, u32[]{:S(2)}, u32[]{:S(2)}) collective-permute-start(f32[8,128]{1,0:T(8,128)S(1)} %get-tuple-element.121), channel_id=1, source_target_pairs={{0,2},{2,0},{4,6},{6,4},{8,10},{10,8},{12,14},{14,12},{16,18},{18,... | collective-permute-start | bytes 12296 | tf_op jit(solution)/shard_map/ppermute | solution.py:500
  45.2 1.5 %collective-permute-done.11.even_ref = f32[8,128]{1,0:T(8,128)S(1)} collective-permute-done((f32[8,128]{1,0:T(8,128)S(1)}, f32[8,128]{1,0:T(8,128)S(1)}, u32[]{:S(2)}, u32[]{:S(2)}) %collective-permute-start.11) | collective-permute-done | bytes 4128 | tf_op jit(solution)/shard_map/ppermute | solution.py:500
  46.7 2.0 %collective-permute-done.12.odd_ref = f32[8,128]{1,0:T(8,128)S(1)} collective-permute-done((f32[8,128]{1,0:T(8,128)S(1)}, f32[8,128]{1,0:T(8,128)S(1)}, u32[]{:S(2)}, u32[]{:S(2)}) %collective-permute-start.12) | collective-permute-done | bytes 4128 | tf_op jit(solution)/shard_map/ppermute | solution.py:502
  48.7 2.0 %step.6 = (f32[32,320]{1,0:T(8,128)S(1)}, bf16[32,768]{1,0:T(8,128)(2,1)S(1)}, bf16[32,768]{1,0:T(8,128)(2,1)S(1)}, f32[8,128]{1,0:T(8,128)S(1)}, f32[8,128]{1,0...) custom-call(s32[1,32]{1,0:T(1,128)S(1)} %get-tuple-element.79.order_ref, s32[2]{0:T(128)S(1)} %pad_add_fusion.place_ref, ...), custom_call_target="tpu_custom_call" | custom-call | tf_op jit(solution)/shard_map/step/pallas_call | solution.py:525
  51.1 2.2 %collective-permute-start.21 = (f32[72,128]{1,0:T(8,128)S(1)}, f32[72,128]{1,0:T(8,128)S(1)}, u32[]{:S(2)}, u32[]{:S(2)}) collective-permute-start(f32[72,128]{1,0:T(8,128)S(1)} %add_add_fusion.1), channel_id=1, source_target_pairs={{0,128},{2,130},{4,132},{6,134},{8,136},{10,138},{12,140},{14,142}... | collective-permute-start | bytes 110600 | tf_op jit(solution)/shard_map/ppermute | solution.py:496
  53.2 4.1 %collective-permute-start.20 = (f32[72,128]{1,0:T(8,128)S(1)}, f32[72,128]{1,0:T(8,128)S(1)}, u32[]{:S(2)}, u32[]{:S(2)}) collective-permute-start(f32[72,128]{1,0:T(8,128)S(1)} %add_add_fusion.1), channel_id=1, source_target_pairs={{0,64},{2,66},{4,68},{6,70},{8,72},{10,74},{12,76},{14,78},{16,80}... | collective-permute-start | bytes 110600 | tf_op jit(solution)/shard_map/ppermute | solution.py:496
  57.4 5.4 %collective-permute-start.17 = (f32[8,128]{1,0:T(8,128)S(1)}, f32[8,128]{1,0:T(8,128)S(1)}, u32[]{:S(2)}, u32[]{:S(2)}) collective-permute-start(f32[8,128]{1,0:T(8,128)S(1)} %get-tuple-element.137), channel_id=1, source_target_pairs={{0,2},{2,0},{4,6},{6,4},{8,10},{10,8},{12,14},{14,12},{16,18},{18,... | collective-permute-start | bytes 12296 | tf_op jit(solution)/shard_map/ppermute | solution.py:500
  62.9 1.5 %collective-permute-done.17.even_ref = f32[8,128]{1,0:T(8,128)S(1)} collective-permute-done((f32[8,128]{1,0:T(8,128)S(1)}, f32[8,128]{1,0:T(8,128)S(1)}, u32[]{:S(2)}, u32[]{:S(2)}) %collective-permute-start.17) | collective-permute-done | bytes 4128 | tf_op jit(solution)/shard_map/ppermute | solution.py:500
  64.4 2.0 %collective-permute-done.18.odd_ref = f32[8,128]{1,0:T(8,128)S(1)} collective-permute-done((f32[8,128]{1,0:T(8,128)S(1)}, f32[8,128]{1,0:T(8,128)S(1)}, u32[]{:S(2)}, u32[]{:S(2)}) %collective-permute-start.18) | collective-permute-done | bytes 4128 | tf_op jit(solution)/shard_map/ppermute | solution.py:502
  66.4 2.3 %step.7 = (f32[16,384]{1,0:T(8,128)S(1)}, f32[16,384]{1,0:T(8,128)S(1)}, f32[32,320]{1,0:T(8,128)}) custom-call(s32[1,32]{1,0:T(1,128)S(1)} %get-tuple-element.79.order_ref, s32[2]{0:T(128)S(1)} %pad_add_fusion.place_ref, f32[32,320]{1,0:T(8,128)S(1)} %get-tuple-element.130.field_ref, bf16[32,768]{1,0:T(8,128)(2,1)S(1)} %get-tuple-element.131.chi_ref, ...), custom_call_target="tpu_custom_call" | custom-call | tf_op jit(solution)/shard_map/step/pallas_call | solution.py:525
  71.4 13.0 %all-to-all-start = ((f32[128,4,128]{2,1,0:T(4,128)}), f32[128,4,128]{2,1,0:T(4,128)S(1)}, u32[]{:S(2)}, u32[]{:S(2)}) async-start(f32[128,4,128]{2,1,0:T(4,128)} %get-tuple-element.148), calls=%async_computation | async-start | bytes 524288 | tf_op jit(solution)/shard_map/all_to_all | solution.py:557
  85.6 3.3 %collective-permute-done.24 = f32[72,128]{1,0:T(8,128)S(1)} collective-permute-done((f32[72,128]{1,0:T(8,128)S(1)}, f32[72,128]{1,0:T(8,128)S(1)}, u32[]{:S(2)}, u32[]{:S(2)}) %collective-permute-start.24) | collective-permute-done | bytes 36896 | tf_op jit(solution)/shard_map/ppermute | solution.py:496
  88.9 9.4 %factor.1 = (f32[128,128]{1,0:T(8,128)S(1)}, f32[128,128]{1,0:T(8,128)S(1)}) custom-call(f32[72,128]{1,0:T(8,128)S(1)} %add.52.gram_ref), custom_call_target="tpu_custom_call" | custom-call | tf_op jit(solution)/shard_map/factor/pallas_call | solution.py:542
  100.7 4.6 %final.1 = f32[2,16,320,128]{3,2,1,0:T(8,128)} custom-call(s32[2]{0:T(128)S(1)} %pad_add_fusion.place_ref, bf16[128,256]{1,0:T(8,128)(2,1)S(1)} %get-tuple-element.152.w_ref, bf16[256,256]{1,0:T(8,128)(2,1)S(1)} %get-tuple-element.153.wf_ref, bf16[320,256]{1,0:T(8,128)(2,1)S(1)} %get-tuple-element.154.turned_ref, ...), custom_call_target="tpu_custom_call" | custom-call | tf_op jit(solution)/shard_map/final/pallas_call | solution.py:567
  (62 shorter events, 11.9 us)
Async XLA Ops:
  2.6 6.4 %collective-permute-start = (f32[8,128]{1,0:T(8,128)S(1)}, f32[8,128]{1,0:T(8,128)S(1)}, u32[]{:S(2)}, u32[]{:S(2)}) collective-permute-start(f32[8,128]{1,0:T(8,128)S(1)} %get-tuple-element.90), channel_id=1, source_target_pairs={{0,2},{2,0},{4,6},{6,4},{8,10},{10,8},{12,14},{14,12},{16,18},{18,... | collective-permute-start | bytes 12296 | tf_op jit(solution)/shard_map/ppermute | solution.py:500
  5.0 4.1 %collective-permute-start.1 = (f32[8,128]{1,0:T(8,128)S(1)}, f32[8,128]{1,0:T(8,128)S(1)}, u32[]{:S(2)}, u32[]{:S(2)}) collective-permute-start(f32[8,128]{1,0:T(8,128)S(1)} %get-tuple-element.91), channel_id=1, source_target_pairs={{0,254},{2,4},{4,2},{6,8},{8,6},{10,12},{12,10},{14,16},{16,14},{1... | collective-permute-start | bytes 12296 | tf_op jit(solution)/shard_map/ppermute | solution.py:502
  5.4 3.7 %collective-permute-start.2 = (f32[8,128]{1,0:T(8,128)S(1)}, f32[8,128]{1,0:T(8,128)S(1)}, u32[]{:S(2)}, u32[]{:S(2)}) collective-permute-start(f32[8,128]{1,0:T(8,128)S(1)} %get-tuple-element.92), channel_id=1, source_target_pairs={{0,1},{1,0},{2,3},{3,2},{4,5},{5,4},{6,7},{7,6},{8,9},{9,8},{10,11... | collective-permute-start | bytes 12296 | tf_op jit(solution)/shard_map/ppermute | solution.py:503
  9.0 21.9 %collective-permute-start.10 = (bf16[16,320,124]{2,1,0:T(8,128)(2,1)S(1)}, bf16[16,320,124]{2,1,0:T(8,128)(2,1)S(1)}, u32[]{:S(2)}, u32[]{:S(2)}) collective-permute-start(bf16[16,320,124]{2,1,0:T(8,128)(2,1)S(1)} %get-tuple-element.109.sent_ref), channel_id=1, source_target_pairs={{0,1},{1,0},{2,3},{3,2},{4,5},{5,4},{6,7},{7,6},{8,9},{9,8},{10,11... | collective-permute-start | bytes 3809288 | tf_op jit(solution)/shard_map/ppermute | solution.py:507
  13.1 14.2 %collective-permute-start.9 = (f32[72,128]{1,0:T(8,128)S(1)}, f32[72,128]{1,0:T(8,128)S(1)}, u32[]{:S(2)}, u32[]{:S(2)}) collective-permute-start(f32[72,128]{1,0:T(8,128)S(1)} %add.42), channel_id=1, source_target_pairs={{0,12},{2,14},{4,8},{6,10},{8,4},{10,6},{12,0},{14,2},{16,28},{18,... | collective-permute-start | bytes 110600 | tf_op jit(solution)/shard_map/ppermute | solution.py:496
  16.6 10.7 %collective-permute-start.8 = (f32[72,128]{1,0:T(8,128)S(1)}, f32[72,128]{1,0:T(8,128)S(1)}, u32[]{:S(2)}, u32[]{:S(2)}) collective-permute-start(f32[72,128]{1,0:T(8,128)S(1)} %add.42), channel_id=1, source_target_pairs={{0,8},{2,10},{4,12},{6,14},{8,0},{10,2},{12,4},{14,6},{16,24},{18,... | collective-permute-start | bytes 110600 | tf_op jit(solution)/shard_map/ppermute | solution.py:496
  17.0 10.4 %collective-permute-start.7 = (f32[72,128]{1,0:T(8,128)S(1)}, f32[72,128]{1,0:T(8,128)S(1)}, u32[]{:S(2)}, u32[]{:S(2)}) collective-permute-start(f32[72,128]{1,0:T(8,128)S(1)} %add.42), channel_id=1, source_target_pairs={{0,4},{2,6},{4,0},{6,2},{8,12},{10,14},{12,8},{14,10},{16,20},{18,... | collective-permute-start | bytes 110600 | tf_op jit(solution)/shard_map/ppermute | solution.py:496
  18.1 11.1 %collective-permute-start.4 = (f32[8,128]{1,0:T(8,128)S(1)}, f32[8,128]{1,0:T(8,128)S(1)}, u32[]{:S(2)}, u32[]{:S(2)}) collective-permute-start(f32[8,128]{1,0:T(8,128)S(1)} %get-tuple-element.105), channel_id=1, source_target_pairs={{0,2},{2,0},{4,6},{6,4},{8,10},{10,8},{12,14},{14,12},{16,18},{18,... | collective-permute-start | bytes 12296 | tf_op jit(solution)/shard_map/ppermute | solution.py:500
  27.3 3.6 %collective-permute-start.5 = (f32[8,128]{1,0:T(8,128)S(1)}, f32[8,128]{1,0:T(8,128)S(1)}, u32[]{:S(2)}, u32[]{:S(2)}) collective-permute-start(f32[8,128]{1,0:T(8,128)S(1)} %get-tuple-element.106), channel_id=1, source_target_pairs={{0,254},{2,4},{4,2},{6,8},{8,6},{10,12},{12,10},{14,16},{16,14},{1... | collective-permute-start | bytes 12296 | tf_op jit(solution)/shard_map/ppermute | solution.py:502
  27.3 3.6 %collective-permute-start.6 = (f32[24,384]{1,0:T(8,128)S(1)}, f32[24,384]{1,0:T(8,128)S(1)}, u32[]{:S(2)}, u32[]{:S(2)}) collective-permute-start(f32[24,384]{1,0:T(8,128)S(1)} %get-tuple-element.107), channel_id=1, source_target_pairs={{0,1},{1,0},{2,3},{3,2},{4,5},{5,4},{6,7},{7,6},{8,9},{9,8},{10,11... | collective-permute-start | bytes 110600 | tf_op jit(solution)/shard_map/ppermute | solution.py:503
  33.0 12.2 %collective-permute-start.16 = (f32[72,128]{1,0:T(8,128)S(1)}, f32[72,128]{1,0:T(8,128)S(1)}, u32[]{:S(2)}, u32[]{:S(2)}) collective-permute-start(f32[72,128]{1,0:T(8,128)S(1)} %add_add_fusion.2), channel_id=1, source_target_pairs={{0,48},{2,50},{4,52},{6,54},{8,56},{10,58},{12,60},{14,62},{16,32}... | collective-permute-start | bytes 110600 | tf_op jit(solution)/shard_map/ppermute | solution.py:496
  33.1 12.1 %collective-permute-start.15 = (f32[72,128]{1,0:T(8,128)S(1)}, f32[72,128]{1,0:T(8,128)S(1)}, u32[]{:S(2)}, u32[]{:S(2)}) collective-permute-start(f32[72,128]{1,0:T(8,128)S(1)} %add_add_fusion.2), channel_id=1, source_target_pairs={{0,32},{2,34},{4,36},{6,38},{8,40},{10,42},{12,44},{14,46},{16,48}... | collective-permute-start | bytes 110600 | tf_op jit(solution)/shard_map/ppermute | solution.py:496
  33.2 12.0 %collective-permute-start.14 = (f32[72,128]{1,0:T(8,128)S(1)}, f32[72,128]{1,0:T(8,128)S(1)}, u32[]{:S(2)}, u32[]{:S(2)}) collective-permute-start(f32[72,128]{1,0:T(8,128)S(1)} %add_add_fusion.2), channel_id=1, source_target_pairs={{0,16},{2,18},{4,20},{6,22},{8,24},{10,26},{12,28},{14,30},{16,0},... | collective-permute-start | bytes 110600 | tf_op jit(solution)/shard_map/ppermute | solution.py:496
  38.0 8.7 %collective-permute-start.11 = (f32[8,128]{1,0:T(8,128)S(1)}, f32[8,128]{1,0:T(8,128)S(1)}, u32[]{:S(2)}, u32[]{:S(2)}) collective-permute-start(f32[8,128]{1,0:T(8,128)S(1)} %get-tuple-element.121), channel_id=1, source_target_pairs={{0,2},{2,0},{4,6},{6,4},{8,10},{10,8},{12,14},{14,12},{16,18},{18,... | collective-permute-start | bytes 12296 | tf_op jit(solution)/shard_map/ppermute | solution.py:500
  45.1 3.6 %collective-permute-start.12 = (f32[8,128]{1,0:T(8,128)S(1)}, f32[8,128]{1,0:T(8,128)S(1)}, u32[]{:S(2)}, u32[]{:S(2)}) collective-permute-start(f32[8,128]{1,0:T(8,128)S(1)} %get-tuple-element.122), channel_id=1, source_target_pairs={{0,254},{2,4},{4,2},{6,8},{8,6},{10,12},{12,10},{14,16},{16,14},{1... | collective-permute-start | bytes 12296 | tf_op jit(solution)/shard_map/ppermute | solution.py:502
  45.1 3.6 %collective-permute-start.13 = (f32[24,384]{1,0:T(8,128)S(1)}, f32[24,384]{1,0:T(8,128)S(1)}, u32[]{:S(2)}, u32[]{:S(2)}) collective-permute-start(f32[24,384]{1,0:T(8,128)S(1)} %get-tuple-element.123), channel_id=1, source_target_pairs={{0,1},{1,0},{2,3},{3,2},{4,5},{5,4},{6,7},{7,6},{8,9},{9,8},{10,11... | collective-permute-start | bytes 110600 | tf_op jit(solution)/shard_map/ppermute | solution.py:503
  50.8 12.0 %collective-permute-start.22 = (f32[72,128]{1,0:T(8,128)S(1)}, f32[72,128]{1,0:T(8,128)S(1)}, u32[]{:S(2)}, u32[]{:S(2)}) collective-permute-start(f32[72,128]{1,0:T(8,128)S(1)} %add_add_fusion.1), channel_id=1, source_target_pairs={{0,192},{2,194},{4,196},{6,198},{8,200},{10,202},{12,204},{14,206}... | collective-permute-start | bytes 110600 | tf_op jit(solution)/shard_map/ppermute | solution.py:496
  51.1 11.7 %collective-permute-start.21 = (f32[72,128]{1,0:T(8,128)S(1)}, f32[72,128]{1,0:T(8,128)S(1)}, u32[]{:S(2)}, u32[]{:S(2)}) collective-permute-start(f32[72,128]{1,0:T(8,128)S(1)} %add_add_fusion.1), channel_id=1, source_target_pairs={{0,128},{2,130},{4,132},{6,134},{8,136},{10,138},{12,140},{14,142}... | collective-permute-start | bytes 110600 | tf_op jit(solution)/shard_map/ppermute | solution.py:496
  53.2 9.6 %collective-permute-start.20 = (f32[72,128]{1,0:T(8,128)S(1)}, f32[72,128]{1,0:T(8,128)S(1)}, u32[]{:S(2)}, u32[]{:S(2)}) collective-permute-start(f32[72,128]{1,0:T(8,128)S(1)} %add_add_fusion.1), channel_id=1, source_target_pairs={{0,64},{2,66},{4,68},{6,70},{8,72},{10,74},{12,76},{14,78},{16,80}... | collective-permute-start | bytes 110600 | tf_op jit(solution)/shard_map/ppermute | solution.py:496
  57.4 7.0 %collective-permute-start.17 = (f32[8,128]{1,0:T(8,128)S(1)}, f32[8,128]{1,0:T(8,128)S(1)}, u32[]{:S(2)}, u32[]{:S(2)}) collective-permute-start(f32[8,128]{1,0:T(8,128)S(1)} %get-tuple-element.137), channel_id=1, source_target_pairs={{0,2},{2,0},{4,6},{6,4},{8,10},{10,8},{12,14},{14,12},{16,18},{18,... | collective-permute-start | bytes 12296 | tf_op jit(solution)/shard_map/ppermute | solution.py:500
  62.8 3.6 %collective-permute-start.18 = (f32[8,128]{1,0:T(8,128)S(1)}, f32[8,128]{1,0:T(8,128)S(1)}, u32[]{:S(2)}, u32[]{:S(2)}) collective-permute-start(f32[8,128]{1,0:T(8,128)S(1)} %get-tuple-element.138), channel_id=1, source_target_pairs={{0,254},{2,4},{4,2},{6,8},{8,6},{10,12},{12,10},{14,16},{16,14},{1... | collective-permute-start | bytes 12296 | tf_op jit(solution)/shard_map/ppermute | solution.py:502
  62.8 3.6 %collective-permute-start.19 = (f32[24,384]{1,0:T(8,128)S(1)}, f32[24,384]{1,0:T(8,128)S(1)}, u32[]{:S(2)}, u32[]{:S(2)}) collective-permute-start(f32[24,384]{1,0:T(8,128)S(1)} %get-tuple-element.139), channel_id=1, source_target_pairs={{0,1},{1,0},{2,3},{3,2},{4,5},{5,4},{6,7},{7,6},{8,9},{9,8},{10,11... | collective-permute-start | bytes 110600 | tf_op jit(solution)/shard_map/ppermute | solution.py:503
  71.4 27.9 %all-to-all-start = ((f32[128,4,128]{2,1,0:T(4,128)}), f32[128,4,128]{2,1,0:T(4,128)S(1)}, u32[]{:S(2)}, u32[]{:S(2)}) async-start(f32[128,4,128]{2,1,0:T(4,128)} %get-tuple-element.148), calls=%async_computation | async-start | bytes 524288 | tf_op jit(solution)/shard_map/all_to_all | solution.py:557
  84.4 4.5 %collective-permute-start.24 = (f32[72,128]{1,0:T(8,128)S(1)}, f32[72,128]{1,0:T(8,128)S(1)}, u32[]{:S(2)}, u32[]{:S(2)}) collective-permute-start(f32[72,128]{1,0:T(8,128)S(1)} %add_add_fusion), channel_id=1, source_target_pairs={{0,2},{2,0},{4,6},{6,4},{8,10},{10,8},{12,14},{14,12},{16,18},{18,... | collective-permute-start | bytes 110600 | tf_op jit(solution)/shard_map/ppermute | solution.py:496
  (6 other events, 12.3 us)

commit v3 on v2

--- a/solution.py
+++ b/solution.py
@@ -256,6 +256,10 @@
     col = iota((SNAPS, SNAPS), 1)
     start = jnp.where((row < HIST) & (col < HIST), unfold(gram_ref[...]) * scale, jnp.where(row == col, 1.0, 0.0))
     ident = jnp.where(row == col, 1.0, 0.0)
+    on = jnp.where(row == col, start, 0.0)
+    across = jnp.sum(on, axis=0, keepdims=True)
+    shrink = 1.0 / jnp.sqrt(across)
+    start = start * (1.0 / jnp.sqrt(jnp.sum(on, axis=1, keepdims=True))) * shrink
     a = [start[8 * t : 8 * t + 8] for t in range(tiles)]
     b = [ident[8 * t : 8 * t + 8] for t in range(tiles)]
     below = iota((8, SNAPS), 0)
@@ -298,8 +302,8 @@
     root = 1.0 / jnp.sqrt(diag - ratio * side)
     up = (up - ratio * pltpu.roll(up, 1, 0)) * root
     low = (low - ratio * pltpu.roll(low, 1, 0)) * root
-    up_ref[...] = jnp.where(col >= row, up, 0.0)
-    inv_ref[...] = jnp.where(col <= row, low, 0.0)
+    up_ref[...] = jnp.where(col >= row, up, 0.0) * (across * shrink)
+    inv_ref[...] = jnp.where(col <= row, low, 0.0) * shrink
 
 
 def rows_kernel(fields_ref, keep_ref, other_ref, out_ref, turned_ref):

time: 106 us -> 106 us (level)
  no operation moved by 1% of the time
where the time goes in v3:
time: 106 us; the launch traced here: 105 us
  starting transfers between devices  56.2 us (53%)
  Pallas kernels  31.2 us (29%)
  waiting for transfers between devices  16 us (15%)
  between operations  1.11 us (1%)
    ppermute x4, starting transfers between devices, body(): even = lax.ppermute(zev, 'solver', evens)  24.1 us
    ppermute x10, starting transfers between devices, summed(): lax.ppermute(gram, 'solver', [(i, i ^ bit) for i in range(groups)])  17.9 us
    all_to_all x1, starting transfers between devices, body(): gathered = lax.all_to_all(rows, 'solver', 0, 0, tiled=True)  13 us
    pallas_call x1, Pallas kernels, body(): pl.pallas_call(functools.partial(factor_kernel, scale), in_specs=[VMEM],...  9.52 us
    pallas_call x4, Pallas kernels, body(): pl.pallas_call(functools.partial(step_kernel, last), in_specs=[SMEM, SMEM...  8.38 us
    ppermute x4, waiting for transfers between devices, body(): odd = lax.ppermute(zod, 'solver', odds)  5.68 us
    ppermute x4, waiting for transfers between devices, body(): even = lax.ppermute(zev, 'solver', evens)  4.89 us
    pallas_call x1, Pallas kernels, body(): pl.pallas_call(final_kernel, in_specs=[SMEM] + [VMEM] * 5, out_specs=ANY,...  4.56 us
  transfers between devices with their start and end apart: 26, of which 9 were waited for; matrix products, arithmetic and copies ran while one was open for 1% of the time, Pallas kernels for 15%

profile of v3, /device:TPU:2, one launch (start us, length us, event | category | flops | bytes accessed | tf_op | source)
XLA Modules:
  0.0 105.5 jit_solution(10831620988625708339)
XLA Ops:
  0.7 1.9 %setup.1 = (bf16[6,32,48]{2,1,0:T(8,128)(2,1)S(1)}, bf16[32,32]{1,0:T(8,128)(2,1)S(1)}, s32[1,32]{1,0:T(1,128)S(1)}, bf16[320,768]{1,0:T(8,128)(2,1)S(1)}, bf16[...) custom-call(s32[1]{0:T(128)} %bitcast.2.base_ref, ...), custom_call_target="tpu_custom_call" | custom-call | tf_op jit(solution)/shard_map/setup/pallas_call | solution.py:441
  2.6 2.4 %collective-permute-start = (f32[8,128]{1,0:T(8,128)S(1)}, f32[8,128]{1,0:T(8,128)S(1)}, u32[]{:S(2)}, u32[]{:S(2)}) collective-permute-start(f32[8,128]{1,0:T(8,128)S(1)} %get-tuple-element.90), channel_id=1, source_target_pairs={{0,2},{2,0},{4,6},{6,4},{8,10},{10,8},{12,14},{14,12},{16,18},{18,... | collective-permute-start | bytes 12296 | tf_op jit(solution)/shard_map/ppermute | solution.py:504
  5.4 2.6 %pick.1 = (bf16[16,320,124]{2,1,0:T(8,128)(2,1)S(1)}, bf16[16,320,124]{2,1,0:T(8,128)(2,1)S(1)}) custom-call(s32[1,32]{1,0:T(1,128)S(1)} %get-tuple-element.79.order_ref, s32[2]{0:T(128)S(1)} %pad_add_fusion.place_ref, bf16[32,320,124]{2,1,0:T(8,128)(2,1)} %bitcast.29), custom_call_target="tpu_custom_call" | custom-call | tf_op jit(solution)/shard_map/pick/pallas_call | solution.py:465
  11.0 2.0 %step.4 = (f32[32,320]{1,0:T(8,128)S(1)}, bf16[32,768]{1,0:T(8,128)(2,1)S(1)}, bf16[32,768]{1,0:T(8,128)(2,1)S(1)}, f32[8,128]{1,0:T(8,128)S(1)}, f32[8,128]{1,0...) custom-call(s32[1,32]{1,0:T(1,128)S(1)} %get-tuple-element.79.order_ref, s32[2]{0:T(128)S(1)} %pad_add_fusion.place_ref, ...), custom_call_target="tpu_custom_call" | custom-call | tf_op jit(solution)/shard_map/step/pallas_call | solution.py:529
  13.1 3.5 %collective-permute-start.9 = (f32[72,128]{1,0:T(8,128)S(1)}, f32[72,128]{1,0:T(8,128)S(1)}, u32[]{:S(2)}, u32[]{:S(2)}) collective-permute-start(f32[72,128]{1,0:T(8,128)S(1)} %add.42), channel_id=1, source_target_pairs={{0,12},{2,14},{4,8},{6,10},{8,4},{10,6},{12,0},{14,2},{16,28},{18,... | collective-permute-start | bytes 110600 | tf_op jit(solution)/shard_map/ppermute | solution.py:500
  18.1 9.2 %collective-permute-start.4 = (f32[8,128]{1,0:T(8,128)S(1)}, f32[8,128]{1,0:T(8,128)S(1)}, u32[]{:S(2)}, u32[]{:S(2)}) collective-permute-start(f32[8,128]{1,0:T(8,128)S(1)} %get-tuple-element.105), channel_id=1, source_target_pairs={{0,2},{2,0},{4,6},{6,4},{8,10},{10,8},{12,14},{14,12},{16,18},{18,... | collective-permute-start | bytes 12296 | tf_op jit(solution)/shard_map/ppermute | solution.py:504
  27.4 1.8 %collective-permute-done.4.even_ref = f32[8,128]{1,0:T(8,128)S(1)} collective-permute-done((f32[8,128]{1,0:T(8,128)S(1)}, f32[8,128]{1,0:T(8,128)S(1)}, u32[]{:S(2)}, u32[]{:S(2)}) %collective-permute-start.4) | collective-permute-done | bytes 4128 | tf_op jit(solution)/shard_map/ppermute | solution.py:504
  29.3 1.6 %collective-permute-done.5.odd_ref = f32[8,128]{1,0:T(8,128)S(1)} collective-permute-done((f32[8,128]{1,0:T(8,128)S(1)}, f32[8,128]{1,0:T(8,128)S(1)}, u32[]{:S(2)}, u32[]{:S(2)}) %collective-permute-start.5) | collective-permute-done | bytes 4128 | tf_op jit(solution)/shard_map/ppermute | solution.py:506
  30.9 2.0 %step.5 = (f32[32,320]{1,0:T(8,128)S(1)}, bf16[32,768]{1,0:T(8,128)(2,1)S(1)}, bf16[32,768]{1,0:T(8,128)(2,1)S(1)}, f32[8,128]{1,0:T(8,128)S(1)}, f32[8,128]{1,0...) custom-call(s32[1,32]{1,0:T(1,128)S(1)} %get-tuple-element.79.order_ref, s32[2]{0:T(128)S(1)} %pad_add_fusion.place_ref, ...), custom_call_target="tpu_custom_call" | custom-call | tf_op jit(solution)/shard_map/step/pallas_call | solution.py:529
  33.2 4.9 %collective-permute-start.14 = (f32[72,128]{1,0:T(8,128)S(1)}, f32[72,128]{1,0:T(8,128)S(1)}, u32[]{:S(2)}, u32[]{:S(2)}) collective-permute-start(f32[72,128]{1,0:T(8,128)S(1)} %add_add_fusion.2), channel_id=1, source_target_pairs={{0,16},{2,18},{4,20},{6,22},{8,24},{10,26},{12,28},{14,30},{16,0},... | collective-permute-start | bytes 110600 | tf_op jit(solution)/shard_map/ppermute | solution.py:500
  38.0 7.1 %collective-permute-start.11 = (f32[8,128]{1,0:T(8,128)S(1)}, f32[8,128]{1,0:T(8,128)S(1)}, u32[]{:S(2)}, u32[]{:S(2)}) collective-permute-start(f32[8,128]{1,0:T(8,128)S(1)} %get-tuple-element.121), channel_id=1, source_target_pairs={{0,2},{2,0},{4,6},{6,4},{8,10},{10,8},{12,14},{14,12},{16,18},{18,... | collective-permute-start | bytes 12296 | tf_op jit(solution)/shard_map/ppermute | solution.py:504
  45.2 1.5 %collective-permute-done.11.even_ref = f32[8,128]{1,0:T(8,128)S(1)} collective-permute-done((f32[8,128]{1,0:T(8,128)S(1)}, f32[8,128]{1,0:T(8,128)S(1)}, u32[]{:S(2)}, u32[]{:S(2)}) %collective-permute-start.11) | collective-permute-done | bytes 4128 | tf_op jit(solution)/shard_map/ppermute | solution.py:504
  46.7 2.0 %collective-permute-done.12.odd_ref = f32[8,128]{1,0:T(8,128)S(1)} collective-permute-done((f32[8,128]{1,0:T(8,128)S(1)}, f32[8,128]{1,0:T(8,128)S(1)}, u32[]{:S(2)}, u32[]{:S(2)}) %collective-permute-start.12) | collective-permute-done | bytes 4128 | tf_op jit(solution)/shard_map/ppermute | solution.py:506
  48.7 2.0 %step.6 = (f32[32,320]{1,0:T(8,128)S(1)}, bf16[32,768]{1,0:T(8,128)(2,1)S(1)}, bf16[32,768]{1,0:T(8,128)(2,1)S(1)}, f32[8,128]{1,0:T(8,128)S(1)}, f32[8,128]{1,0...) custom-call(s32[1,32]{1,0:T(1,128)S(1)} %get-tuple-element.79.order_ref, s32[2]{0:T(128)S(1)} %pad_add_fusion.place_ref, ...), custom_call_target="tpu_custom_call" | custom-call | tf_op jit(solution)/shard_map/step/pallas_call | solution.py:529
  51.1 2.2 %collective-permute-start.21 = (f32[72,128]{1,0:T(8,128)S(1)}, f32[72,128]{1,0:T(8,128)S(1)}, u32[]{:S(2)}, u32[]{:S(2)}) collective-permute-start(f32[72,128]{1,0:T(8,128)S(1)} %add_add_fusion.1), channel_id=1, source_target_pairs={{0,128},{2,130},{4,132},{6,134},{8,136},{10,138},{12,140},{14,142}... | collective-permute-start | bytes 110600 | tf_op jit(solution)/shard_map/ppermute | solution.py:500
  53.2 4.1 %collective-permute-start.20 = (f32[72,128]{1,0:T(8,128)S(1)}, f32[72,128]{1,0:T(8,128)S(1)}, u32[]{:S(2)}, u32[]{:S(2)}) collective-permute-start(f32[72,128]{1,0:T(8,128)S(1)} %add_add_fusion.1), channel_id=1, source_target_pairs={{0,64},{2,66},{4,68},{6,70},{8,72},{10,74},{12,76},{14,78},{16,80}... | collective-permute-start | bytes 110600 | tf_op jit(solution)/shard_map/ppermute | solution.py:500
  57.4 5.4 %collective-permute-start.17 = (f32[8,128]{1,0:T(8,128)S(1)}, f32[8,128]{1,0:T(8,128)S(1)}, u32[]{:S(2)}, u32[]{:S(2)}) collective-permute-start(f32[8,128]{1,0:T(8,128)S(1)} %get-tuple-element.137), channel_id=1, source_target_pairs={{0,2},{2,0},{4,6},{6,4},{8,10},{10,8},{12,14},{14,12},{16,18},{18,... | collective-permute-start | bytes 12296 | tf_op jit(solution)/shard_map/ppermute | solution.py:504
  62.9 1.5 %collective-permute-done.17.even_ref = f32[8,128]{1,0:T(8,128)S(1)} collective-permute-done((f32[8,128]{1,0:T(8,128)S(1)}, f32[8,128]{1,0:T(8,128)S(1)}, u32[]{:S(2)}, u32[]{:S(2)}) %collective-permute-start.17) | collective-permute-done | bytes 4128 | tf_op jit(solution)/shard_map/ppermute | solution.py:504
  64.4 2.0 %collective-permute-done.18.odd_ref = f32[8,128]{1,0:T(8,128)S(1)} collective-permute-done((f32[8,128]{1,0:T(8,128)S(1)}, f32[8,128]{1,0:T(8,128)S(1)}, u32[]{:S(2)}, u32[]{:S(2)}) %collective-permute-start.18) | collective-permute-done | bytes 4128 | tf_op jit(solution)/shard_map/ppermute | solution.py:506
  66.4 2.3 %step.7 = (f32[16,384]{1,0:T(8,128)S(1)}, f32[16,384]{1,0:T(8,128)S(1)}, f32[32,320]{1,0:T(8,128)}) custom-call(s32[1,32]{1,0:T(1,128)S(1)} %get-tuple-element.79.order_ref, s32[2]{0:T(128)S(1)} %pad_add_fusion.place_ref, f32[32,320]{1,0:T(8,128)S(1)} %get-tuple-element.130.field_ref, bf16[32,768]{1,0:T(8,128)(2,1)S(1)} %get-tuple-element.131.chi_ref, ...), custom_call_target="tpu_custom_call" | custom-call | tf_op jit(solution)/shard_map/step/pallas_call | solution.py:529
  71.4 13.0 %all-to-all-start = ((f32[128,4,128]{2,1,0:T(4,128)}), f32[128,4,128]{2,1,0:T(4,128)S(1)}, u32[]{:S(2)}, u32[]{:S(2)}) async-start(f32[128,4,128]{2,1,0:T(4,128)} %get-tuple-element.148), calls=%async_computation | async-start | bytes 524288 | tf_op jit(solution)/shard_map/all_to_all | solution.py:561
  85.6 3.3 %collective-permute-done.24 = f32[72,128]{1,0:T(8,128)S(1)} collective-permute-done((f32[72,128]{1,0:T(8,128)S(1)}, f32[72,128]{1,0:T(8,128)S(1)}, u32[]{:S(2)}, u32[]{:S(2)}) %collective-permute-start.24) | collective-permute-done | bytes 36896 | tf_op jit(solution)/shard_map/ppermute | solution.py:500
  88.9 9.5 %factor.1 = (f32[128,128]{1,0:T(8,128)S(1)}, f32[128,128]{1,0:T(8,128)S(1)}) custom-call(f32[72,128]{1,0:T(8,128)S(1)} %add.52.gram_ref), custom_call_target="tpu_custom_call" | custom-call | tf_op jit(solution)/shard_map/factor/pallas_call | solution.py:546
  100.7 4.6 %final.1 = f32[2,16,320,128]{3,2,1,0:T(8,128)} custom-call(s32[2]{0:T(128)S(1)} %pad_add_fusion.place_ref, bf16[128,256]{1,0:T(8,128)(2,1)S(1)} %get-tuple-element.152.w_ref, bf16[256,256]{1,0:T(8,128)(2,1)S(1)} %get-tuple-element.153.wf_ref, bf16[320,256]{1,0:T(8,128)(2,1)S(1)} %get-tuple-element.154.turned_ref, ...), custom_call_target="tpu_custom_call" | custom-call | tf_op jit(solution)/shard_map/final/pallas_call | solution.py:571
  (62 shorter events, 11.8 us)
Async XLA Ops:
  2.6 6.4 %collective-permute-start = (f32[8,128]{1,0:T(8,128)S(1)}, f32[8,128]{1,0:T(8,128)S(1)}, u32[]{:S(2)}, u32[]{:S(2)}) collective-permute-start(f32[8,128]{1,0:T(8,128)S(1)} %get-tuple-element.90), channel_id=1, source_target_pairs={{0,2},{2,0},{4,6},{6,4},{8,10},{10,8},{12,14},{14,12},{16,18},{18,... | collective-permute-start | bytes 12296 | tf_op jit(solution)/shard_map/ppermute | solution.py:504
  5.0 4.1 %collective-permute-start.1 = (f32[8,128]{1,0:T(8,128)S(1)}, f32[8,128]{1,0:T(8,128)S(1)}, u32[]{:S(2)}, u32[]{:S(2)}) collective-permute-start(f32[8,128]{1,0:T(8,128)S(1)} %get-tuple-element.91), channel_id=1, source_target_pairs={{0,254},{2,4},{4,2},{6,8},{8,6},{10,12},{12,10},{14,16},{16,14},{1... | collective-permute-start | bytes 12296 | tf_op jit(solution)/shard_map/ppermute | solution.py:506
  5.4 3.7 %collective-permute-start.2 = (f32[8,128]{1,0:T(8,128)S(1)}, f32[8,128]{1,0:T(8,128)S(1)}, u32[]{:S(2)}, u32[]{:S(2)}) collective-permute-start(f32[8,128]{1,0:T(8,128)S(1)} %get-tuple-element.92), channel_id=1, source_target_pairs={{0,1},{1,0},{2,3},{3,2},{4,5},{5,4},{6,7},{7,6},{8,9},{9,8},{10,11... | collective-permute-start | bytes 12296 | tf_op jit(solution)/shard_map/ppermute | solution.py:507
  9.0 21.9 %collective-permute-start.10 = (bf16[16,320,124]{2,1,0:T(8,128)(2,1)S(1)}, bf16[16,320,124]{2,1,0:T(8,128)(2,1)S(1)}, u32[]{:S(2)}, u32[]{:S(2)}) collective-permute-start(bf16[16,320,124]{2,1,0:T(8,128)(2,1)S(1)} %get-tuple-element.109.sent_ref), channel_id=1, source_target_pairs={{0,1},{1,0},{2,3},{3,2},{4,5},{5,4},{6,7},{7,6},{8,9},{9,8},{10,11... | collective-permute-start | bytes 3809288 | tf_op jit(solution)/shard_map/ppermute | solution.py:511
  13.1 14.3 %collective-permute-start.9 = (f32[72,128]{1,0:T(8,128)S(1)}, f32[72,128]{1,0:T(8,128)S(1)}, u32[]{:S(2)}, u32[]{:S(2)}) collective-permute-start(f32[72,128]{1,0:T(8,128)S(1)} %add.42), channel_id=1, source_target_pairs={{0,12},{2,14},{4,8},{6,10},{8,4},{10,6},{12,0},{14,2},{16,28},{18,... | collective-permute-start | bytes 110600 | tf_op jit(solution)/shard_map/ppermute | solution.py:500
  16.6 10.7 %collective-permute-start.8 = (f32[72,128]{1,0:T(8,128)S(1)}, f32[72,128]{1,0:T(8,128)S(1)}, u32[]{:S(2)}, u32[]{:S(2)}) collective-permute-start(f32[72,128]{1,0:T(8,128)S(1)} %add.42), channel_id=1, source_target_pairs={{0,8},{2,10},{4,12},{6,14},{8,0},{10,2},{12,4},{14,6},{16,24},{18,... | collective-permute-start | bytes 110600 | tf_op jit(solution)/shard_map/ppermute | solution.py:500
  17.0 10.4 %collective-permute-start.7 = (f32[72,128]{1,0:T(8,128)S(1)}, f32[72,128]{1,0:T(8,128)S(1)}, u32[]{:S(2)}, u32[]{:S(2)}) collective-permute-start(f32[72,128]{1,0:T(8,128)S(1)} %add.42), channel_id=1, source_target_pairs={{0,4},{2,6},{4,0},{6,2},{8,12},{10,14},{12,8},{14,10},{16,20},{18,... | collective-permute-start | bytes 110600 | tf_op jit(solution)/shard_map/ppermute | solution.py:500
  18.1 11.1 %collective-permute-start.4 = (f32[8,128]{1,0:T(8,128)S(1)}, f32[8,128]{1,0:T(8,128)S(1)}, u32[]{:S(2)}, u32[]{:S(2)}) collective-permute-start(f32[8,128]{1,0:T(8,128)S(1)} %get-tuple-element.105), channel_id=1, source_target_pairs={{0,2},{2,0},{4,6},{6,4},{8,10},{10,8},{12,14},{14,12},{16,18},{18,... | collective-permute-start | bytes 12296 | tf_op jit(solution)/shard_map/ppermute | solution.py:504
  27.3 3.6 %collective-permute-start.5 = (f32[8,128]{1,0:T(8,128)S(1)}, f32[8,128]{1,0:T(8,128)S(1)}, u32[]{:S(2)}, u32[]{:S(2)}) collective-permute-start(f32[8,128]{1,0:T(8,128)S(1)} %get-tuple-element.106), channel_id=1, source_target_pairs={{0,254},{2,4},{4,2},{6,8},{8,6},{10,12},{12,10},{14,16},{16,14},{1... | collective-permute-start | bytes 12296 | tf_op jit(solution)/shard_map/ppermute | solution.py:506
  27.3 3.6 %collective-permute-start.6 = (f32[24,384]{1,0:T(8,128)S(1)}, f32[24,384]{1,0:T(8,128)S(1)}, u32[]{:S(2)}, u32[]{:S(2)}) collective-permute-start(f32[24,384]{1,0:T(8,128)S(1)} %get-tuple-element.107), channel_id=1, source_target_pairs={{0,1},{1,0},{2,3},{3,2},{4,5},{5,4},{6,7},{7,6},{8,9},{9,8},{10,11... | collective-permute-start | bytes 110600 | tf_op jit(solution)/shard_map/ppermute | solution.py:507
  33.0 12.2 %collective-permute-start.16 = (f32[72,128]{1,0:T(8,128)S(1)}, f32[72,128]{1,0:T(8,128)S(1)}, u32[]{:S(2)}, u32[]{:S(2)}) collective-permute-start(f32[72,128]{1,0:T(8,128)S(1)} %add_add_fusion.2), channel_id=1, source_target_pairs={{0,48},{2,50},{4,52},{6,54},{8,56},{10,58},{12,60},{14,62},{16,32}... | collective-permute-start | bytes 110600 | tf_op jit(solution)/shard_map/ppermute | solution.py:500
  33.1 12.1 %collective-permute-start.15 = (f32[72,128]{1,0:T(8,128)S(1)}, f32[72,128]{1,0:T(8,128)S(1)}, u32[]{:S(2)}, u32[]{:S(2)}) collective-permute-start(f32[72,128]{1,0:T(8,128)S(1)} %add_add_fusion.2), channel_id=1, source_target_pairs={{0,32},{2,34},{4,36},{6,38},{8,40},{10,42},{12,44},{14,46},{16,48}... | collective-permute-start | bytes 110600 | tf_op jit(solution)/shard_map/ppermute | solution.py:500
  33.2 12.0 %collective-permute-start.14 = (f32[72,128]{1,0:T(8,128)S(1)}, f32[72,128]{1,0:T(8,128)S(1)}, u32[]{:S(2)}, u32[]{:S(2)}) collective-permute-start(f32[72,128]{1,0:T(8,128)S(1)} %add_add_fusion.2), channel_id=1, source_target_pairs={{0,16},{2,18},{4,20},{6,22},{8,24},{10,26},{12,28},{14,30},{16,0},... | collective-permute-start | bytes 110600 | tf_op jit(solution)/shard_map/ppermute | solution.py:500
  38.0 8.7 %collective-permute-start.11 = (f32[8,128]{1,0:T(8,128)S(1)}, f32[8,128]{1,0:T(8,128)S(1)}, u32[]{:S(2)}, u32[]{:S(2)}) collective-permute-start(f32[8,128]{1,0:T(8,128)S(1)} %get-tuple-element.121), channel_id=1, source_target_pairs={{0,2},{2,0},{4,6},{6,4},{8,10},{10,8},{12,14},{14,12},{16,18},{18,... | collective-permute-start | bytes 12296 | tf_op jit(solution)/shard_map/ppermute | solution.py:504
  45.1 3.6 %collective-permute-start.12 = (f32[8,128]{1,0:T(8,128)S(1)}, f32[8,128]{1,0:T(8,128)S(1)}, u32[]{:S(2)}, u32[]{:S(2)}) collective-permute-start(f32[8,128]{1,0:T(8,128)S(1)} %get-tuple-element.122), channel_id=1, source_target_pairs={{0,254},{2,4},{4,2},{6,8},{8,6},{10,12},{12,10},{14,16},{16,14},{1... | collective-permute-start | bytes 12296 | tf_op jit(solution)/shard_map/ppermute | solution.py:506
  45.1 3.6 %collective-permute-start.13 = (f32[24,384]{1,0:T(8,128)S(1)}, f32[24,384]{1,0:T(8,128)S(1)}, u32[]{:S(2)}, u32[]{:S(2)}) collective-permute-start(f32[24,384]{1,0:T(8,128)S(1)} %get-tuple-element.123), channel_id=1, source_target_pairs={{0,1},{1,0},{2,3},{3,2},{4,5},{5,4},{6,7},{7,6},{8,9},{9,8},{10,11... | collective-permute-start | bytes 110600 | tf_op jit(solution)/shard_map/ppermute | solution.py:507
  50.8 12.0 %collective-permute-start.22 = (f32[72,128]{1,0:T(8,128)S(1)}, f32[72,128]{1,0:T(8,128)S(1)}, u32[]{:S(2)}, u32[]{:S(2)}) collective-permute-start(f32[72,128]{1,0:T(8,128)S(1)} %add_add_fusion.1), channel_id=1, source_target_pairs={{0,192},{2,194},{4,196},{6,198},{8,200},{10,202},{12,204},{14,206}... | collective-permute-start | bytes 110600 | tf_op jit(solution)/shard_map/ppermute | solution.py:500
  51.1 11.7 %collective-permute-start.21 = (f32[72,128]{1,0:T(8,128)S(1)}, f32[72,128]{1,0:T(8,128)S(1)}, u32[]{:S(2)}, u32[]{:S(2)}) collective-permute-start(f32[72,128]{1,0:T(8,128)S(1)} %add_add_fusion.1), channel_id=1, source_target_pairs={{0,128},{2,130},{4,132},{6,134},{8,136},{10,138},{12,140},{14,142}... | collective-permute-start | bytes 110600 | tf_op jit(solution)/shard_map/ppermute | solution.py:500
  53.2 9.6 %collective-permute-start.20 = (f32[72,128]{1,0:T(8,128)S(1)}, f32[72,128]{1,0:T(8,128)S(1)}, u32[]{:S(2)}, u32[]{:S(2)}) collective-permute-start(f32[72,128]{1,0:T(8,128)S(1)} %add_add_fusion.1), channel_id=1, source_target_pairs={{0,64},{2,66},{4,68},{6,70},{8,72},{10,74},{12,76},{14,78},{16,80}... | collective-permute-start | bytes 110600 | tf_op jit(solution)/shard_map/ppermute | solution.py:500
  57.4 7.0 %collective-permute-start.17 = (f32[8,128]{1,0:T(8,128)S(1)}, f32[8,128]{1,0:T(8,128)S(1)}, u32[]{:S(2)}, u32[]{:S(2)}) collective-permute-start(f32[8,128]{1,0:T(8,128)S(1)} %get-tuple-element.137), channel_id=1, source_target_pairs={{0,2},{2,0},{4,6},{6,4},{8,10},{10,8},{12,14},{14,12},{16,18},{18,... | collective-permute-start | bytes 12296 | tf_op jit(solution)/shard_map/ppermute | solution.py:504
  62.8 3.6 %collective-permute-start.18 = (f32[8,128]{1,0:T(8,128)S(1)}, f32[8,128]{1,0:T(8,128)S(1)}, u32[]{:S(2)}, u32[]{:S(2)}) collective-permute-start(f32[8,128]{1,0:T(8,128)S(1)} %get-tuple-element.138), channel_id=1, source_target_pairs={{0,254},{2,4},{4,2},{6,8},{8,6},{10,12},{12,10},{14,16},{16,14},{1... | collective-permute-start | bytes 12296 | tf_op jit(solution)/shard_map/ppermute | solution.py:506
  62.8 3.6 %collective-permute-start.19 = (f32[24,384]{1,0:T(8,128)S(1)}, f32[24,384]{1,0:T(8,128)S(1)}, u32[]{:S(2)}, u32[]{:S(2)}) collective-permute-start(f32[24,384]{1,0:T(8,128)S(1)} %get-tuple-element.139), channel_id=1, source_target_pairs={{0,1},{1,0},{2,3},{3,2},{4,5},{5,4},{6,7},{7,6},{8,9},{9,8},{10,11... | collective-permute-start | bytes 110600 | tf_op jit(solution)/shard_map/ppermute | solution.py:507
  71.4 27.9 %all-to-all-start = ((f32[128,4,128]{2,1,0:T(4,128)}), f32[128,4,128]{2,1,0:T(4,128)S(1)}, u32[]{:S(2)}, u32[]{:S(2)}) async-start(f32[128,4,128]{2,1,0:T(4,128)} %get-tuple-element.148), calls=%async_computation | async-start | bytes 524288 | tf_op jit(solution)/shard_map/all_to_all | solution.py:561
  84.4 4.5 %collective-permute-start.24 = (f32[72,128]{1,0:T(8,128)S(1)}, f32[72,128]{1,0:T(8,128)S(1)}, u32[]{:S(2)}, u32[]{:S(2)}) collective-permute-start(f32[72,128]{1,0:T(8,128)S(1)} %add_add_fusion), channel_id=1, source_target_pairs={{0,2},{2,0},{4,6},{6,4},{8,10},{10,8},{12,14},{14,12},{16,18},{18,... | collective-permute-start | bytes 110600 | tf_op jit(solution)/shard_map/ppermute | solution.py:500
  (6 other events, 12.3 us)
